TPU v7x, 256 devices: a whole 4x4x8 slice. The times are simulated.
256 devices in a mesh: gx: 8 (over y_hi, x), gy: 32 (over y_lo, z, core).
Axes of the slice: x: 4, y: 4 (y_hi: 2, y_lo: 2; y = y_hi * 2 + y_lo), z: 8, core: 2. Of those that a mesh axis runs over, the one named last changes fastest.
Arguments:
- velocity: float32 [3, 8, 32, 8192], P(None, 'gx', 'gy'), may hold values from -6 to 6
- position: float32 [3, 8, 32, 8192], P(None, 'gx', 'gy'), may hold values from -0.5 to 128, as said below
- leaving: int32 [8, 32, 4], P('gx', 'gy'), may hold values from 256 to 1024, as said below
- grid_shift: int32 [3], replicated, may hold values from 1 to 3
- axis_index: int32 [8, 32, 8192], P('gx', 'gy'), may hold values from 0 to 15
Outputs:
- new_velocity: float32 [3, 8, 32, 12288], P(None, 'gx', 'gy')
- cell_flow: float32 [3, 8, 32, 8192], P(None, 'gx', 'gy')
Inputs may be any that keep to these rules, and one draw needn't show every extreme that they name: leaving[i, j] counts the rows of tile (i, j) that leave across its lower x, upper x, lower y and upper y side, laid out from row 0 in that order; the y counts exclude rows that leave across an x side. Each x run holds at most 128 rows that also leave across the lower y side and at most 128 across the upper. Counting the rows that arrive from an x neighbour and go on, at most 1024 particles cross any side of a tile; in every draw some tile sends exactly 1024 across its lower x side and exactly 1024 across its lower y side, and some x runs hold exactly 128 such rows. `position`: positions are in cell units of the holding tile's frame and multiples of 1/4096, with z in [0, 128). Rows past the four runs have x in [0, 8) and y in [0, 8). A row of an x run lies less than 0.5 outside the tile on its side in x, with y inside or, for a corner row, less than 0.5 outside; a row of a y run has x inside and y less than 0.5 outside on its side.
All inputs are finite; a program needn't handle non-finite values.
Results may differ from a plain program's by a relative error of at most 0.0003.
Values sent between devices are 32-bit elements; how exact they have to be, the bound alone decides.
A program may use at most 64 MiB of HBM per device.

v0:
```python
import jax
import jax.numpy as jnp
from jax import lax
from jax.sharding import PartitionSpec as P

CXL = 8
CYL = 8
CZ = 128
NAX = 16
MIG = 1024


COS_TURN = -0.6427876096865393
SIN_TURN = 0.766044443118978
GOLDEN_TURN = 2.399963229728653
SENTINEL = -1000.0


def extended(block, sides, width):
    for axis, dim in sides:
        count = lax.axis_size(axis)
        forward = [(i, i + 1) for i in range(count - 1)]
        forward.append((count - 1, 0))
        backward = [(target, source) for source, target in forward]
        low = lax.ppermute(
            lax.slice_in_dim(block, block.shape[dim] - width, None, axis=dim), axis, forward
        )
        high = lax.ppermute(lax.slice_in_dim(block, 0, width, axis=dim), axis, backward)
        block = jnp.concatenate([low, block, high], axis=dim)
    return block


def axis_table():
    number = jnp.arange(NAX).astype(jnp.float32)
    height = 1.0 - (2.0 * number + 1.0) / NAX
    radius = jnp.sqrt(1.0 - height * height)
    phase = number * GOLDEN_TURN
    return jnp.stack([radius * jnp.cos(phase), radius * jnp.sin(phase), height])


def empty_slots(width):
    return jnp.concatenate(
        [jnp.zeros((3, width), jnp.float32), jnp.full((3, width), SENTINEL, jnp.float32)], 0
    )


def take_run(particle_rows, start, count):
    block_rows = lax.dynamic_slice_in_dim(particle_rows, start, MIG, 1)
    slot_live = jnp.arange(MIG, dtype=jnp.int32) < count
    return jnp.where(slot_live[None, :], block_rows, empty_slots(1))


def is_live(buffer):
    return buffer[3] > -100.0


def place(base_rows, base_count, arrivals, chosen, width):
    flags = chosen.astype(jnp.int32)
    rank_ids = jnp.cumsum(flags) - flags
    slot_ids = jnp.where(chosen, base_count + rank_ids, width)
    return base_rows.at[:, slot_ids].set(arrivals, mode="drop")


def cell_ids(particle_rows, living, grid_shift):
    extent = (CXL + 1) * (CYL + 1) * CZ
    sub_cells = jnp.floor(4.0 * particle_rows[3:6]).astype(jnp.int32)
    cell_x = (sub_cells[0] + grid_shift[0]) // 4
    cell_y = (sub_cells[1] + grid_shift[1]) // 4
    cell_z = (sub_cells[2] + grid_shift[2]) // 4 % CZ
    flat_ids = (cell_x * (CYL + 1) + cell_y) * CZ + cell_z
    return jnp.where(living, flat_ids, extent)


def rotate(velocity_rows, mean_rows, axis_rows, living):
    relative = velocity_rows - mean_rows
    cross = jnp.stack(
        [
            axis_rows[1] * relative[2] - axis_rows[2] * relative[1],
            axis_rows[2] * relative[0] - axis_rows[0] * relative[2],
            axis_rows[0] * relative[1] - axis_rows[1] * relative[0],
        ]
    )
    along = jnp.sum(axis_rows * relative, axis=0)
    turned = (
        mean_rows
        + COS_TURN * relative
        + SIN_TURN * cross
        + (1.0 - COS_TURN) * along[None, :] * axis_rows
    )
    return jnp.where(living[None, :], turned, 0.0)


def per_device(velocity, position, leaving, grid_shift, axis_index):
    extent = (CXL + 1) * (CYL + 1) * CZ
    particle_rows = jnp.concatenate([velocity.reshape(3, -1), position.reshape(3, -1)], 0)
    moving = leaving.reshape(4)
    low_x = take_run(particle_rows, 0, moving[0])
    high_x = take_run(particle_rows, moving[0], moving[1])
    low_y_run = take_run(particle_rows, moving[0] + moving[1], moving[2])
    high_y_run = take_run(particle_rows, moving[0] + moving[1] + moving[2], moving[3])
    got_x = extended(jnp.concatenate([low_x, high_x], 1), (("gx", 1),), MIG)
    arrivals = jnp.concatenate(
        [got_x[:, :MIG].at[3].add(-float(CXL)), got_x[:, 3 * MIG :].at[3].add(float(CXL))], 1
    )
    arrive_live = is_live(arrivals)
    downward = arrive_live & (arrivals[4] < 0.0)
    upward = arrive_live & (arrivals[4] >= CYL)
    staying = arrive_live & jnp.logical_not(downward) & jnp.logical_not(upward)
    send_y = jnp.concatenate(
        [
            place(low_y_run, moving[2], arrivals, downward, MIG),
            place(high_y_run, moving[3], arrivals, upward, MIG),
        ],
        1,
    )
    got_y = extended(send_y, (("gy", 1),), MIG)
    from_below = got_y[:, :MIG]
    from_above = got_y[:, 3 * MIG :]
    from_below = from_below.at[4].add(-float(CYL))
    from_above = from_above.at[4].add(float(CYL))
    own_live = (
        jnp.arange(particle_rows.shape[1], dtype=jnp.int32)
        >= moving[0] + moving[1] + moving[2] + moving[3]
    )
    settled = jnp.concatenate([particle_rows, arrivals, from_below, from_above], 1)
    living = jnp.concatenate([own_live, staying, is_live(from_below), is_live(from_above)])
    flat_ids = cell_ids(settled, living, grid_shift)
    weights = jnp.stack([jnp.ones_like(settled[0]), settled[0], settled[1], settled[2]], 1)
    sums = jax.ops.segment_sum(weights, flat_ids, num_segments=extent + 1)[:extent]
    sums = sums.T.reshape(4, CXL + 1, CYL + 1, CZ)
    table = axis_table()
    picked = jnp.sum(
        jnp.where(
            axis_index == jnp.arange(NAX, dtype=jnp.int32)[None, :, None], table[:, :, None], 0.0
        ),
        axis=1,
    )
    own_axes = jnp.pad(picked.reshape(3, CXL, CYL, CZ), ((0, 0), (0, 1), (0, 1), (0, 0)))
    stacked = jnp.concatenate([sums, own_axes], 0)
    rims = extended(stacked, (("gx", 1), ("gy", 2)), 1)
    total = rims[:, 1:-1, 1:-1]
    total = total.at[:, 0].add(rims[:, 0, 1:-1])
    total = total.at[:, -1].add(rims[:, -1, 1:-1])
    total = total.at[:, :, 0].add(rims[:, 1:-1, 0])
    total = total.at[:, :, -1].add(rims[:, 1:-1, -1])
    total = total.at[:, 0, 0].add(rims[:, 0, 0])
    total = total.at[:, 0, -1].add(rims[:, 0, -1])
    total = total.at[:, -1, 0].add(rims[:, -1, 0])
    total = total.at[:, -1, -1].add(rims[:, -1, -1])
    mean_cells = total[1:4] / jnp.maximum(total[0:1], 1.0)
    row_table = jnp.concatenate([mean_cells, total[4:7]], 0).reshape(6, extent).T
    looked = row_table[jnp.minimum(flat_ids, extent - 1)].T
    new_velocity = rotate(settled[0:3], looked[0:3], looked[3:6], living)
    cell_flow = mean_cells[:, :CXL, :CYL].reshape(3, 1, 1, -1)
    return (new_velocity.reshape(3, 1, 1, -1), cell_flow)


def solution(mesh):
    return jax.shard_map(
        per_device,
        mesh=mesh,
        in_specs=(
            P(None, "gx", "gy", None),
            P(None, "gx", "gy", None),
            P("gx", "gy", None),
            P(),
            P("gx", "gy", None),
        ),
        out_specs=(P(None, "gx", "gy", None), P(None, "gx", "gy", None)),
        check_vma=False,
    )
```

profile of v0, /device:TPU:6, one launch (start us, length us, event | category | flops | bytes accessed | tf_op | source)
XLA Modules:
  0.0 217.0 jit_solution(4803608542367245918)
XLA Ops:
  0.6 1.5 fusion.42
  5.3 1.3 iota_compare_fusion.4
  11.3 4.8 %collective-permute-start = (f32[6,1024]{1,0:T(8,128)S(1)}, f32[6,1024]{1,0:T(8,128)S(1)}, u32[]{:S(2)}, u32[]{:S(2)}) collective-permute-start(f32[6,1024]{1,0:T(8,128)S(1)} %get-tuple-element.180), channel_id=1, source_target_pairs={{0,32},{32,64},{64,96},{96,128},{128,160},{160,192},{192,224},{224... | collective-permute-start | bytes 73736 | tf_op jit(solution)/shard_map/ppermute | solution.py:25
  16.9 1.4 fusion.41
  19.5 1.3 and_reduce_fusion
  23.9 1.3 compare_select_fusion.12
  25.3 5.8 %scatter_fusion.1 = f32[6,1024]{0,1:T(8,128)S(1)} fusion(f32[6,1024]{0,1:T(8,128)S(1)} %copy.98, s32[2048]{0:T(1024)S(1)} %bitcast.100, f32[2048,6]{1,0:T(8,128)S(1)} %copy.96), kind=kCustom, calls=%fused_computation.2 | custom fusion | bytes 155648 | tf_op jit(solution)/shard_map/scatter | solution.py:61
  31.3 5.8 %collective-permute-start.3 = (f32[6,1024]{1,0:T(8,128)S(1)}, f32[6,1024]{1,0:T(8,128)S(1)}, u32[]{:S(2)}, u32[]{:S(2)}) collective-permute-start(f32[6,1024]{1,0:T(8,128)S(1)} %copy.100), channel_id=1, source_target_pairs={{1,0},{2,1},{3,2},{4,3},{5,4},{6,5},{7,6},{8,7},{9,8},{10,9},{11,1... | collective-permute-start | bytes 73736 | tf_op jit(solution)/shard_map/ppermute | solution.py:28
  37.1 5.8 %scatter_fusion = f32[6,1024]{0,1:T(8,128)S(1)} fusion(f32[6,1024]{0,1:T(8,128)S(1)} %copy.95, s32[2048]{0:T(1024)S(1)} %bitcast.99, f32[2048,6]{1,0:T(8,128)S(1)} %copy.96), kind=kCustom, calls=%fused_computation.1 | custom fusion | bytes 155648 | tf_op jit(solution)/shard_map/scatter | solution.py:61
  43.2 5.4 %collective-permute-done.2 = f32[6,1024]{1,0:T(8,128)S(1)} collective-permute-done((f32[6,1024]{1,0:T(8,128)S(1)}, f32[6,1024]{1,0:T(8,128)S(1)}, u32[]{:S(2)}, u32[]{:S(2)}) %collective-permute-start.2) | collective-permute-done | bytes 24608 | tf_op jit(solution)/shard_map/ppermute | solution.py:25
  49.5 4.0 %copy.101 = f32[12288,4]{1,0:T(8,128)} copy(f32[12288,4]{0,1:T(4,128)S(1)} %pad_maximum_fusion.3) | data formatting | bytes 393216 | tf_op jit(solution)/shard_map/stack | solution.py:128
  53.5 2.9 %compare_select_fusion = (s32[12288,1]{0,1:T(1,128)S(1)}, s32[12288,1]{0,1:T(1,128)S(1)}) fusion(s32[]{:T(128)} %bitcast.19, s32[3,12288]{1,0:T(4,128)S(1)} %fusion.4, s32[]{:T(128)} %bitcast.17, s32[]{:T(128)} %bitcast.15, pred[1024,1]{0,1:T(4,128)(4,1)S(1)} %get-tuple-element.188, pred[1024,1]{0,1:T(4,128)(4,1)S(1)} %get-tuple-element.186, ...), kind=kLoop, calls=%fused_computation.23 | loop fusion | flops 872448 | bytes 258060 | tf_op jit(solution)/shard_map/select_n | solution.py:152
  56.4 76.1 %scatter_custom_fusion.2 = f32[10369,4]{1,0:T(8,128)} fusion(s32[12288]{0:T(1024)S(1)} %bitcast.98, f32[12288,4]{1,0:T(8,128)} %copy.101, f32[]{:T(128)} %constant.391.clone.1), kind=kCustom, calls=%fused_computation.4 | custom fusion | flops 49152 | bytes 166416 | tf_op jit(solution)/shard_map/scatter-add | solution.py:129
  132.5 4.2 %slice.542 = f32[10368,4]{1,0:T(8,128)} slice(f32[10369,4]{1,0:T(8,128)} %scatter_custom_fusion.2), slice={[0:10368], [0:4]} | slice | bytes 331776 | tf_op jit(solution)/shard_map/slice | solution.py:129
  136.7 5.0 %copy.107 = f32[4,9,9,128]{3,2,1,0:T(8,128)S(1)} copy(f32[4,9,9,128]{0,3,2,1:T(8,128)} %bitcast.90) | data formatting | bytes 331776 | tf_op jit(solution)/shard_map/reshape | solution.py:130
  141.7 1.4 collective-permute-start.4
  143.2 2.8 %collective-permute-done.4 = f32[7,1,9,128]{3,2,1,0:T(8,128)S(1)} collective-permute-done((f32[7,1,9,128]{3,2,1,0:T(8,128)S(1)}, f32[7,1,9,128]{3,2,1,0:T(8,128)S(1)}, u32[]{:S(2)}, u32[]{:S(2)}) %collective-permute-start.4) | collective-permute-done | bytes 32288 | tf_op jit(solution)/shard_map/ppermute | solution.py:25
  146.1 7.8 %collective-permute-done.5 = f32[7,1,9,128]{3,2,1,0:T(8,128)S(1)} collective-permute-done((f32[7,1,9,128]{3,2,1,0:T(8,128)S(1)}, f32[7,1,9,128]{3,2,1,0:T(8,128)S(1)}, u32[]{:S(2)}, u32[]{:S(2)}) %collective-permute-start.5) | collective-permute-done | bytes 32288 | tf_op jit(solution)/shard_map/ppermute | solution.py:28
  154.0 3.8 %collective-permute-start.7 = (f32[7,11,1,128]{3,2,1,0:T(1,128)S(1)}, f32[7,11,1,128]{3,2,1,0:T(1,128)S(1)}, u32[]{:S(2)}, u32[]{:S(2)}) collective-permute-start(f32[7,11,1,128]{3,2,1,0:T(1,128)S(1)} %get-tuple-element.169), channel_id=1, source_target_pairs={{1,0},{2,1},{3,2},{4,3},{5,4},{6,5},{7,6},{8,7},{9,8},{10,9},{11,1... | collective-permute-start | bytes 118280 | tf_op jit(solution)/shard_map/ppermute | solution.py:28
  157.9 1.6 collective-permute-done.6
  160.0 1.8 broadcast_select_fusion
  163.9 3.6 %copy.103 = f32[6,9,9,128]{0,3,2,1:T(8,128)} copy(f32[6,9,9,128]{3,2,1,0:T(8,128)S(1)} %pad_maximum_fusion.2) | data formatting | bytes 497664 | tf_op jit(solution)/shard_map/concatenate | solution.py:151
  167.5 43.5 %gather_fusion = f32[12288,6]{1,0:T(8,128)} fusion(f32[10368,6]{1,0:T(8,128)} %bitcast.89, s32[12288]{0:T(1024)S(1)} %broadcast_clamp_fusion), kind=kCustom, calls=%fused_computation | custom fusion | bytes 638976 | tf_op jit(solution)/shard_map/gather | solution.py:152
  211.0 4.4 %copy.104 = f32[12288,6]{0,1:T(8,128)S(1)} copy(f32[12288,6]{1,0:T(8,128)} %gather_fusion) | data formatting | bytes 589824 | tf_op jit(solution)/shard_map/gather | solution.py:152
  (88 shorter events, 14.0 us)
Async XLA Ops:
  10.4 11.6 %collective-permute-start.1 = (f32[6,1024]{1,0:T(8,128)S(1)}, f32[6,1024]{1,0:T(8,128)S(1)}, u32[]{:S(2)}, u32[]{:S(2)}) collective-permute-start(f32[6,1024]{1,0:T(8,128)S(1)} %get-tuple-element.181), channel_id=1, source_target_pairs={{32,0},{64,32},{96,64},{128,96},{160,128},{192,160},{224,192},{0,2... | collective-permute-start | bytes 73736 | tf_op jit(solution)/shard_map/ppermute | solution.py:28
  11.3 10.7 %collective-permute-start = (f32[6,1024]{1,0:T(8,128)S(1)}, f32[6,1024]{1,0:T(8,128)S(1)}, u32[]{:S(2)}, u32[]{:S(2)}) collective-permute-start(f32[6,1024]{1,0:T(8,128)S(1)} %get-tuple-element.180), channel_id=1, source_target_pairs={{0,32},{32,64},{64,96},{96,128},{128,160},{160,192},{192,224},{224... | collective-permute-start | bytes 73736 | tf_op jit(solution)/shard_map/ppermute | solution.py:25
  31.3 17.4 %collective-permute-start.3 = (f32[6,1024]{1,0:T(8,128)S(1)}, f32[6,1024]{1,0:T(8,128)S(1)}, u32[]{:S(2)}, u32[]{:S(2)}) collective-permute-start(f32[6,1024]{1,0:T(8,128)S(1)} %copy.100), channel_id=1, source_target_pairs={{1,0},{2,1},{3,2},{4,3},{5,4},{6,5},{7,6},{8,7},{9,8},{10,9},{11,1... | collective-permute-start | bytes 73736 | tf_op jit(solution)/shard_map/ppermute | solution.py:28
  43.1 5.5 %collective-permute-start.2 = (f32[6,1024]{1,0:T(8,128)S(1)}, f32[6,1024]{1,0:T(8,128)S(1)}, u32[]{:S(2)}, u32[]{:S(2)}) collective-permute-start(f32[6,1024]{1,0:T(8,128)S(1)} %copy.97), channel_id=1, source_target_pairs={{0,1},{1,2},{2,3},{3,4},{4,5},{5,6},{6,7},{7,8},{8,9},{9,10},{10,1... | collective-permute-start | bytes 73736 | tf_op jit(solution)/shard_map/ppermute | solution.py:25
  141.7 4.3 %collective-permute-start.4 = (f32[7,1,9,128]{3,2,1,0:T(8,128)S(1)}, f32[7,1,9,128]{3,2,1,0:T(8,128)S(1)}, u32[]{:S(2)}, u32[]{:S(2)}) collective-permute-start(f32[7,1,9,128]{3,2,1,0:T(8,128)S(1)} %fusion.12), channel_id=1, source_target_pairs={{0,32},{32,64},{64,96},{96,128},{128,160},{160,192},{192,224},{224... | collective-permute-start | bytes 96776 | tf_op jit(solution)/shard_map/ppermute | solution.py:25
  146.0 7.9 %collective-permute-start.5 = (f32[7,1,9,128]{3,2,1,0:T(8,128)S(1)}, f32[7,1,9,128]{3,2,1,0:T(8,128)S(1)}, u32[]{:S(2)}, u32[]{:S(2)}) collective-permute-start(f32[7,1,9,128]{3,2,1,0:T(8,128)S(1)} %get-tuple-element.165), channel_id=1, source_target_pairs={{32,0},{64,32},{96,64},{128,96},{160,128},{192,160},{224,192},{0,2... | collective-permute-start | bytes 96776 | tf_op jit(solution)/shard_map/ppermute | solution.py:28
  153.9 5.6 %collective-permute-start.6 = (f32[7,11,1,128]{3,2,1,0:T(1,128)S(1)}, f32[7,11,1,128]{3,2,1,0:T(1,128)S(1)}, u32[]{:S(2)}, u32[]{:S(2)}) collective-permute-start(f32[7,11,1,128]{3,2,1,0:T(1,128)S(1)} %get-tuple-element.170), channel_id=1, source_target_pairs={{0,1},{1,2},{2,3},{3,4},{4,5},{5,6},{6,7},{7,8},{8,9},{9,10},{10,1... | collective-permute-start | bytes 118280 | tf_op jit(solution)/shard_map/ppermute | solution.py:25
  154.0 5.7 %collective-permute-start.7 = (f32[7,11,1,128]{3,2,1,0:T(1,128)S(1)}, f32[7,11,1,128]{3,2,1,0:T(1,128)S(1)}, u32[]{:S(2)}, u32[]{:S(2)}) collective-permute-start(f32[7,11,1,128]{3,2,1,0:T(1,128)S(1)} %get-tuple-element.169), channel_id=1, source_target_pairs={{1,0},{2,1},{3,2},{4,3},{5,4},{6,5},{7,6},{8,7},{9,8},{10,9},{11,1... | collective-permute-start | bytes 118280 | tf_op jit(solution)/shard_map/ppermute | solution.py:28
where the time goes:
time: 218 us; the launch traced here: 217 us
  other arithmetic  90.4 us (41%)
  local copies, waits for them, and re-layouts  86.3 us (40%)
  waiting for transfers between devices  17.6 us (8%)
  starting transfers between devices  17 us (8%)
  between operations  5.67 us (3%)
    scatter-add x1, other arithmetic, per_device(): jax.ops.segment_sum(weights, flat_ids, num_segments=extent + 1)[:extent]  76.1 us
    gather x2, local copies, waits for them, and re-layouts, per_device(): looked = row_table[jnp.minimum(flat_ids, extent - 1)].T  47.9 us
    scatter x4, local copies, waits for them, and re-layouts, place(): return base_rows.at[:, slot_ids].set(arrivals, mode='drop')  12 us
    ppermute x4, starting transfers between devices, extended(): lax.ppermute(lax.slice_in_dim(block, 0, width, axis=dim), axis, backward)  10.6 us
    ppermute x4, waiting for transfers between devices, extended(): lax.ppermute(lax.slice_in_dim(block, block.shape[dim] - width, None, axis...  9.78 us
    ppermute x4, waiting for transfers between devices, extended(): lax.ppermute(lax.slice_in_dim(block, 0, width, axis=dim), axis, backward)  7.77 us
    ppermute x4, starting transfers between devices, extended(): lax.ppermute(lax.slice_in_dim(block, block.shape[dim] - width, None, axis...  6.4 us
    reshape x1, local copies, waits for them, and re-layouts, per_device(): sums = sums.T.reshape(4, CXL + 1, CYL + 1, CZ)  4.95 us
  transfers between devices with their start and end apart: 8, of which 4 were waited for; matrix products, arithmetic and copies ran while one was open for 5% of the time, Pallas kernels for 0%

commit v1 on v0

v1 whole, which is shorter than its diff:
```python
import math

import jax
import jax.numpy as jnp
from jax import lax
from jax.experimental import pallas as pl
from jax.experimental.pallas import tpu as pltpu
from jax.sharding import PartitionSpec as P

CXL = 8
CYL = 8
CZ = 128
NAX = 16
MIG = 1024
ROWS = 64
SLOTS = 96
GRID = 10
HALF = GRID // 2
CELL_ROWS = GRID * HALF
PAD_ROWS = 56
SIDE_ROWS = 136
CORNER_ROWS = 24
PLANES = 10

COS_TURN = -0.6427876096865393
SIN_TURN = 0.766044443118978
GOLDEN_TURN = 2.399963229728653

F32 = jnp.float32
BF16 = jnp.bfloat16
MESH = pl.DeviceIdType.MESH


def axis_table():
    table = []
    for number in range(NAX):
        height = 1.0 - (2.0 * number + 1.0) / NAX
        radius = math.sqrt(1.0 - height * height)
        phase = number * GOLDEN_TURN
        table.append((radius * math.cos(phase), radius * math.sin(phase), height))
    return table


def split(value):
    high = value.astype(BF16)
    return high, (value - high.astype(F32)).astype(BF16)


def dot_nt(a, b):
    return lax.dot_general(a, b, (((1,), (1,)), ((), ())), preferred_element_type=F32)


def iota(shape, dim):
    return lax.broadcasted_iota(jnp.int32, shape, dim)


def prep_kernel(
    leaving, shift, vel, pos, axis, side, corner, grid, ids, row_s, col_s, a_s, b_s, sums, run_s, prep_s
):
    shifts = [shift[k].astype(F32) * 0.25 for k in range(3)]
    low_x = (shift[0] == 1).astype(jnp.int32)
    low_y = (shift[1] == 1).astype(jnp.int32)
    cell_x = jnp.floor(pos[0] + shifts[0]) + low_x.astype(F32)
    cell_y = jnp.floor(pos[1] + shifts[1]) + low_y.astype(F32)
    cell_z = jnp.floor(pos[2] + shifts[2])
    cell_z = jnp.where(cell_z >= float(CZ), cell_z - float(CZ), cell_z)
    half = jnp.floor(cell_y * 0.5)
    row = cell_x * float(HALF) + half
    col = (cell_y - 2.0 * half) * float(CZ) + cell_z
    row_s[...] = row
    col_s[...] = col
    ids[...] = row * 256.0 + col

    row_of = iota((64, 128), 0).astype(F32).astype(BF16)
    col_of = iota((256, 128), 0).astype(F32).astype(BF16)
    zero = jnp.zeros((64, 128), BF16)
    one = jnp.ones((64, 128), BF16)
    for chunk in range(8):
        for j in range(8):
            r = chunk * 8 + j
            lanes = slice(j * 128, (j + 1) * 128)
            hit = row_of == jnp.broadcast_to(row_s[r : r + 1, :], (64, 128)).astype(BF16)
            a_s[0:64, lanes] = jnp.where(hit, one, zero)
            for c in range(3):
                high, low = split(vel[c, r : r + 1, :])
                high = jnp.broadcast_to(high.astype(F32), (64, 128)).astype(BF16)
                low = jnp.broadcast_to(low.astype(F32), (64, 128)).astype(BF16)
                at = 64 + 128 * c
                a_s[at : at + 64, lanes] = jnp.where(hit, high, zero)
                a_s[at + 64 : at + 128, lanes] = jnp.where(hit, low, zero)
            hit = col_of == jnp.broadcast_to(col_s[r : r + 1, :], (256, 128)).astype(BF16)
            b_s[:, lanes] = jnp.where(hit, jnp.ones((256, 128), BF16), jnp.zeros((256, 128), BF16))
        part = dot_nt(a_s[...], b_s[...])
        if chunk == 0:
            sums[...] = part
        else:
            sums[...] += part
    for par in range(2):
        lanes = slice(par * 128, (par + 1) * 128)
        grid[par] = sums[0:PAD_ROWS, lanes]
        for c in range(3):
            at = 64 + 128 * c
            grid[2 + 2 * c + par] = sums[at : at + PAD_ROWS, lanes] + sums[at + 64 : at + 64 + PAD_ROWS, lanes]
        grid[8 + par] = jnp.zeros((PAD_ROWS, 128), F32)
    for cx in range(CXL):
        base = (cx + low_x) * HALF
        grid[8 + low_y, pl.ds(base, 4), :] = axis[pl.ds(cx * 8, 4, stride=2), :].astype(F32)
        grid[9 - low_y, pl.ds(base + low_y, 4), :] = axis[pl.ds(cx * 8 + 1, 4, stride=2), :].astype(F32)
    for p in range(PLANES):
        at = slice(p * 10, p * 10 + 10)
        side[0, at, :] = grid[p, 0:10, :]
        side[1, at, :] = grid[p, 40:50, :]
        side[2, at, :] = grid[p, pl.ds(0, 10, stride=5), :]
        side[3, at, :] = grid[p, pl.ds(4, 10, stride=5), :]
        for k, start in enumerate((0, 4, 40, 44)):
            corner[k, p * 2 : p * 2 + 2, :] = grid[p, pl.ds(start, 2, stride=5), :]
    for d in range(4):
        side[d, 100:104, :] = jnp.zeros((4, 128), F32)

    slot = iota((8, 128), 0) * 128 + iota((8, 128), 1)
    lane = iota((8, 128), 1)
    counts = [leaving[k] for k in range(4)]
    starts = [jnp.int32(0), counts[0], counts[0] + counts[1], counts[0] + counts[1] + counts[2]]

    def run(load, d):
        if d == 0:
            return load(0)
        q = starts[d] // 128
        r = starts[d] - q * 128
        back = jnp.where(r == 0, 0, 128 - r)
        here = pltpu.roll(load(q), back, 1)
        after = pltpu.roll(load(q + 1), back, 1)
        return jnp.where(lane < 128 - r, here, after)

    moves = (40.0, -40.0, 4.0, -4.0)
    flags = []
    for d in range(4):
        live = slot < counts[d]
        values = [run(lambda q, c=c: vel[c, pl.ds(q, 8), :], d) for c in range(3)]
        run_id = run(lambda q: ids[pl.ds(q, 8), :], d)
        kept = live
        if d < 2:
            y = run(lambda q: pos[1, pl.ds(q, 8), :], d)
            down = live & (y < 0.0)
            up = live & (y >= float(CYL))
            kept = live & (y >= 0.0) & (y < float(CYL))
            flags += [down, up]
            for c in range(3):
                high = values[c].astype(BF16).astype(F32)
                run_s[d, 16 * c : 16 * c + 8, :] = high
                run_s[d, 16 * c + 8 : 16 * c + 16, :] = values[c] - high
            run_row = jnp.floor(run_id * (1.0 / 256.0))
            run_s[d, 48:56, :] = run_row
            run_s[d, 56:64, :] = run_id - run_row * 256.0
            run_s[d, 64:72, :] = jnp.ones((8, 128), F32)
            run_s[d, 72:128, :] = jnp.zeros((56, 128), F32)
        for c in range(3):
            side[d, 104 + 8 * c : 112 + 8 * c, :] = values[c]
        side[d, 128:136, :] = jnp.where(kept, run_id + moves[d] * 256.0, -1.0)

    flag = jnp.concatenate([f.astype(F32) for f in flags], 0)
    flag16 = flag.astype(BF16)
    before = (iota((128, 128), 0) < iota((128, 128), 1)).astype(F32).astype(BF16)
    inside = jnp.dot(flag16, before, preferred_element_type=F32)
    total = jnp.dot(flag16, jnp.ones((128, 128), BF16), preferred_element_type=F32)
    r0, r1 = iota((32, 32), 0), iota((32, 32), 1)
    earlier = ((r1 < r0) & (r0 // 8 == r1 // 8)).astype(F32).astype(BF16)
    offset = jnp.dot(earlier, total.astype(BF16), preferred_element_type=F32)
    rank = jnp.where(flag > 0.0, inside + offset, -1.0)
    prep_s[...] = rank
    rank_of = iota((128, 128), 0).astype(F32).astype(BF16)
    for d in range(2):
        rows = jnp.concatenate(
            [run_s[d, pl.ds(r, 16, stride=8), :] for r in range(8)], 1
        ).astype(BF16)
        for s in range(2):
            at = d * 16 + s * 8
            hits = []
            for r in range(8):
                hit = rank_of == jnp.broadcast_to(prep_s[at + r : at + r + 1, :], (128, 128)).astype(BF16)
                hits.append(jnp.where(hit, jnp.ones((128, 128), BF16), jnp.zeros((128, 128), BF16)))
            packed = dot_nt(rows, jnp.concatenate(hits, 1))
            k = d * 2 + s
            for c in range(3):
                corner[k, 20 + c : 21 + c, :] = packed[2 * c : 2 * c + 1] + packed[2 * c + 1 : 2 * c + 2]
            moved = packed[6:7] * 256.0 + packed[7:8] + (moves[d] + moves[2 + s]) * 256.0
            corner[k, 23:24, :] = jnp.where(packed[8:9] > 0.5, moved, -1.0)


def exchange_kernel(side, corner, got_side, got_corner, send_side, recv_side, send_corner, recv_corner):
    x, y = lax.axis_index("gx"), lax.axis_index("gy")
    nx, ny = lax.axis_size("gx"), lax.axis_size("gy")
    left, right = lax.rem(x + nx - 1, nx), lax.rem(x + 1, nx)
    down, up = lax.rem(y + ny - 1, ny), lax.rem(y + 1, ny)
    sides = [(left, y), (right, y), (x, down), (x, up)]
    corners = [(left, down), (left, up), (right, down), (right, up)]
    barrier = pltpu.get_barrier_semaphore()
    for target in sides + corners:
        pl.semaphore_signal(barrier, inc=1, device_id=target, device_id_type=MESH)
    pl.semaphore_wait(barrier, 8)
    copies = []
    for k in range(4):
        copies.append(
            pltpu.make_async_remote_copy(
                src_ref=side.at[k],
                dst_ref=got_side.at[k],
                send_sem=send_side.at[k],
                recv_sem=recv_side.at[k],
                device_id=sides[k],
                device_id_type=MESH,
            )
        )
        copies.append(
            pltpu.make_async_remote_copy(
                src_ref=corner.at[k],
                dst_ref=got_corner.at[k],
                send_sem=send_corner.at[k],
                recv_sem=recv_corner.at[k],
                device_id=corners[k],
                device_id_type=MESH,
            )
        )
    for copy in copies:
        copy.start()
    for copy in copies:
        copy.wait()


def collide_kernel(
    leaving, shift, vel, ids, grid, side, corner, out, flow, total, table, slot_v, slot_id, found
):
    low_x = (shift[0] == 1).astype(jnp.int32)
    low_y = (shift[1] == 1).astype(jnp.int32)
    total[...] = grid[...]
    for p in range(PLANES):
        at = slice(p * 10, p * 10 + 10)
        total[p, 0:10, :] += side[1, at, :]
        total[p, 40:50, :] += side[0, at, :]
        total[p, pl.ds(0, 10, stride=5), :] += side[3, at, :]
        total[p, pl.ds(4, 10, stride=5), :] += side[2, at, :]
        for k, start in ((3, 0), (2, 4), (1, 40), (0, 44)):
            total[p, pl.ds(start, 2, stride=5), :] += corner[k, p * 2 : p * 2 + 2, :]
    table[...] = jnp.zeros((256, 512), BF16)
    for par in range(2):
        most = jnp.maximum(total[par], 1.0)
        lanes = slice(par * 128, par * 128 + 128)
        lanes_low = slice(256 + par * 128, 384 + par * 128)
        pad = jnp.zeros((64 - PAD_ROWS, 128), F32)
        for c in range(3):
            mean = total[2 + 2 * c + par] / most
            total[2 + 2 * c + par] = mean
            high, low = split(jnp.concatenate([mean, pad], 0))
            table[64 * c : 64 * c + 64, lanes] = high
            table[64 * c : 64 * c + 64, lanes_low] = low
        table[192:256, lanes] = jnp.concatenate([total[8 + par], pad], 0).astype(BF16)
    for cx in range(CXL):
        base = (cx + low_x) * HALF
        for c in range(3):
            flow[c, pl.ds(cx * 8, 4, stride=2), :] = total[2 + 2 * c + low_y, pl.ds(base, 4), :]
            flow[c, pl.ds(cx * 8 + 1, 4, stride=2), :] = total[
                3 + 2 * c - low_y, pl.ds(base + low_y, 4), :
            ]

    slot = iota((8, 128), 0) * 128 + iota((8, 128), 1)
    for c in range(3):
        slot_v[c, 0:ROWS, :] = vel[c]
        slot_v[c, 64:72, :] = side[1, 104 + 8 * c : 112 + 8 * c, :]
        slot_v[c, 72:80, :] = side[0, 104 + 8 * c : 112 + 8 * c, :]
    gone = leaving[0] + leaving[1] + leaving[2] + leaving[3]
    place = iota((ROWS, 128), 0) * 128 + iota((ROWS, 128), 1)
    slot_id[0:ROWS, :] = jnp.where(place >= gone, ids[...], -1.0)
    slot_id[64:72, :] = side[1, 128:136, :]
    slot_id[72:80, :] = side[0, 128:136, :]
    for at, d, first, second in ((80, 3, 3, 1), (88, 2, 2, 0)):
        run_id = side[d, 128:136, :]
        n0 = jnp.sum((run_id >= 0.0).astype(jnp.int32))
        n1 = jnp.sum((corner[first, 23:24, :] >= 0.0).astype(jnp.int32))
        in_first = (slot >= n0) & (slot < n0 + n1)
        in_second = slot >= n0 + n1
        turn = lax.rem(n0, 128)
        turn2 = lax.rem(n0 + n1, 128)
        in_second = in_second & (slot < n0 + n1 + 128)
        for c in range(4):
            row = 20 + c
            one = pltpu.roll(jnp.broadcast_to(corner[first, row : row + 1, :], (8, 128)), turn, 1)
            two = pltpu.roll(jnp.broadcast_to(corner[second, row : row + 1, :], (8, 128)), turn2, 1)
            base = side[d, 104 + 8 * c : 112 + 8 * c, :]
            merged = jnp.where(in_first, one, jnp.where(in_second, two, base))
            if c < 3:
                slot_v[c, at : at + 8, :] = merged
            else:
                slot_id[at : at + 8, :] = merged

    col_of = iota((256, 128), 0).astype(F32).astype(BF16)
    row_of = iota((PAD_ROWS, 128), 0).astype(F32)
    out[:, 0:8, :] = jnp.zeros((3, 8, 128), F32)

    def group(b, carry):
        at = pl.multiple_of(8 + b * 8, 8)
        block = slot_id[pl.ds(at, 8), :]
        rows = jnp.floor(block * (1.0 / 256.0))
        cols = block - rows * 256.0
        looked = [[], [], [], []]
        for j in range(0, 8, 2):
            hits = []
            for i in (j, j + 1):
                hit = col_of == jnp.broadcast_to(cols[i : i + 1, :], (256, 128)).astype(BF16)
                hits.append(jnp.where(hit, jnp.ones((256, 128), BF16), jnp.zeros((256, 128), BF16)))
            hits = jnp.concatenate(hits, 1)
            both = jnp.dot(
                table[...], jnp.concatenate([hits, hits], 0), preferred_element_type=F32
            )
            for i in (0, 1):
                hit = row_of == jnp.broadcast_to(rows[j + i : j + i + 1, :], (PAD_ROWS, 128))
                for c in range(4):
                    part = both[64 * c : 64 * c + PAD_ROWS, i * 128 : i * 128 + 128]
                    looked[c].append(jnp.sum(jnp.where(hit, part, 0.0), axis=0, keepdims=True))
        mean = [jnp.concatenate(looked[c], 0) for c in range(3)]
        number = jnp.concatenate(looked[3], 0).astype(jnp.int32)
        bits = [(number & (1 << k)) != 0 for k in range(4)]
        turn_axis = []
        for c in range(3):
            level = [row[c] for row in axis_table()]
            for k in range(4):
                level = [
                    jnp.where(bits[k], level[2 * m + 1], level[2 * m]) for m in range(len(level) // 2)
                ]
            turn_axis.append(level[0])
        live = block >= 0.0
        w = [slot_v[c, pl.ds(at, 8), :] - mean[c] for c in range(3)]
        a = turn_axis
        cross = [
            a[1] * w[2] - a[2] * w[1],
            a[2] * w[0] - a[0] * w[2],
            a[0] * w[1] - a[1] * w[0],
        ]
        along = (a[0] * w[0] + a[1] * w[1] + a[2] * w[2]) * (1.0 - COS_TURN)
        for c in range(3):
            turned = mean[c] + COS_TURN * w[c] + SIN_TURN * cross[c] + along * a[c]
            out[c, pl.ds(at, 8), :] = jnp.where(live, turned, 0.0)
        return carry

    lax.fori_loop(0, 11, group, 0)


def per_device(velocity, position, leaving, grid_shift, axis_index):
    vel = velocity.reshape(3, ROWS, 128)
    pos = position.reshape(3, ROWS, 128)
    axis = axis_index.reshape(64, 128)
    leaving = leaving.reshape(4)
    vmem = pl.BlockSpec(memory_space=pltpu.VMEM)
    smem = pl.BlockSpec(memory_space=pltpu.SMEM)
    anywhere = pl.BlockSpec(memory_space=pl.ANY)
    side_shape = jax.ShapeDtypeStruct((4, SIDE_ROWS, 128), F32)
    corner_shape = jax.ShapeDtypeStruct((4, CORNER_ROWS, 128), F32)
    side, corner, grid, ids = pl.pallas_call(
        prep_kernel,
        name="prep",
        out_shape=(
            side_shape,
            corner_shape,
            jax.ShapeDtypeStruct((PLANES, PAD_ROWS, 128), F32),
            jax.ShapeDtypeStruct((ROWS, 128), F32),
        ),
        in_specs=[smem, smem, vmem, vmem, vmem],
        out_specs=(vmem, vmem, vmem, vmem),
        scratch_shapes=[
            pltpu.VMEM((ROWS, 128), F32),
            pltpu.VMEM((ROWS, 128), F32),
            pltpu.VMEM((448, 1024), BF16),
            pltpu.VMEM((256, 1024), BF16),
            pltpu.VMEM((448, 256), F32),
            pltpu.VMEM((2, 128, 128), F32),
            pltpu.VMEM((32, 128), F32),
        ],
        compiler_params=pltpu.CompilerParams(vmem_limit_bytes=32 << 20),
    )(leaving, grid_shift, vel, pos, axis)
    got_side, got_corner = pl.pallas_call(
        exchange_kernel,
        name="exchange",
        out_shape=(side_shape, corner_shape),
        in_specs=[anywhere, anywhere],
        out_specs=(anywhere, anywhere),
        scratch_shapes=[pltpu.SemaphoreType.DMA((4,)) for _ in range(4)],
        compiler_params=pltpu.CompilerParams(collective_id=0, has_side_effects=True),
    )(side, corner)
    out, flow = pl.pallas_call(
        collide_kernel,
        name="collide",
        out_shape=(
            jax.ShapeDtypeStruct((3, SLOTS, 128), F32),
            jax.ShapeDtypeStruct((3, 64, 128), F32),
        ),
        in_specs=[smem, smem, vmem, vmem, vmem, vmem, vmem],
        out_specs=(vmem, vmem),
        scratch_shapes=[
            pltpu.VMEM((PLANES, PAD_ROWS, 128), F32),
            pltpu.VMEM((256, 512), BF16),
            pltpu.VMEM((3, SLOTS, 128), F32),
            pltpu.VMEM((SLOTS, 128), F32),
            pltpu.VMEM((4, SLOTS, 128), F32),
        ],
        compiler_params=pltpu.CompilerParams(vmem_limit_bytes=32 << 20),
    )(leaving, grid_shift, vel, ids, grid, got_side, got_corner)
    return out.reshape(3, 1, 1, SLOTS * 128), flow.reshape(3, 1, 1, 64 * 128)


def solution(mesh):
    return jax.shard_map(
        per_device,
        mesh=mesh,
        in_specs=(
            P(None, "gx", "gy", None),
            P(None, "gx", "gy", None),
            P("gx", "gy", None),
            P(),
            P("gx", "gy", None),
        ),
        out_specs=(P(None, "gx", "gy", None), P(None, "gx", "gy", None)),
        check_vma=False,
    )
```

time: 218 us -> 34.6 us (0.16)
  the two profiles are of different devices: /device:TPU:6 before, /device:TPU:1 now
where the time goes in v1:
time: 34.6 us; the launch traced here: 34.2 us
  Pallas kernels  27.3 us (79%)
  local copies, waits for them, and re-layouts  6.28 us (18%)
  between operations  0.68 us (2%)
    pallas_call x1, Pallas kernels, per_device(): pl.pallas_call(exchange_kernel, name='exchange', out_shape=(side_shape, c...  15.7 us
    pallas_call x1, Pallas kernels, per_device(): pl.pallas_call(collide_kernel, name='collide', out_shape=(jax.ShapeDtypeS...  6.78 us
    unnamed x20, local copies, waits for them, and re-layouts  6.28 us
    pallas_call x1, Pallas kernels, per_device(): pl.pallas_call(prep_kernel, name='prep', out_shape=(side_shape, corner_sh...  4.85 us

profile of v1, /device:TPU:1, one launch (start us, length us, event | category | flops | bytes accessed | tf_op | source)
XLA Modules:
  0.0 34.2 jit_solution(16943318627306500046)
XLA Ops:
  0.6 0.0 copy-start.8
  0.6 0.0 copy-start.9
  0.7 0.6 %copy-done.8 = s32[1,1,4]{2,1,0:T(1,128)S(1)} copy-done((s32[1,1,4]{2,1,0:T(1,128)S(1)}, s32[1,1,4]{2,1,0:T(1,128)}, u32[]{:S(2)}) %copy-start.8) | copy-done | bytes 40
  1.3 0.0 copy-done.9
  1.3 0.0 copy-start
  1.3 0.9 %copy-done = f32[3,1,1,8192]{3,2,1,0:T(1,128)S(1)} copy-done((f32[3,1,1,8192]{3,2,1,0:T(1,128)S(1)}, f32[3,1,1,8192]{3,2,1,0:T(1,128)}, u32[]{:S(2)}) %copy-start) | copy-done | bytes 98328
  2.2 0.0 copy-start.4
  2.2 0.9 %copy-done.4 = f32[3,1,1,8192]{3,2,1,0:T(1,128)S(1)} copy-done((f32[3,1,1,8192]{3,2,1,0:T(1,128)S(1)}, f32[3,1,1,8192]{3,2,1,0:T(1,128)}, u32[]{:S(2)}) %copy-start.4) | copy-done | bytes 98328
  3.1 0.0 copy-start.7
  3.1 0.8 %copy-done.7 = s32[1,1,8192]{2,1,0:T(1,128)S(1)} copy-done((s32[1,1,8192]{2,1,0:T(1,128)S(1)}, s32[1,1,8192]{2,1,0:T(1,128)}, u32[]{:S(2)}) %copy-start.7) | copy-done | bytes 32792
  3.8 4.9 %prep.1 = (f32[4,136,128]{2,1,0:T(8,128)S(1)}, f32[4,24,128]{2,1,0:T(8,128)S(1)}, f32[10,56,128]{2,1,0:T(8,128)S(1)}, f32[64,128]{1,0:T(8,128)S(1)}) custom-call(s32[4]{0:T(128)S(1)} %bitcast.10, s32[3]{0:T(128)S(1)} %copy-done.9, f32[3,64,128]{2,1,0:T(8,128)S(1)} %bitcast.6, f32[3,64,128]{2,1,0:T(8,128)S(1)} %bitcast.8, s32[64,128]{1,0:T(8,128)S(1)} %bitcast.9), custom_call_target="tpu_custom_call" | custom-call | tf_op jit(solution)/shard_map/prep/pallas_call | solution.py:356
  8.7 0.0 copy-start.2
  8.7 0.7 %copy-done.2 = f32[4,136,128]{2,1,0:T(8,128)} copy-done((f32[4,136,128]{2,1,0:T(8,128)}, f32[4,136,128]{2,1,0:T(8,128)S(1)}, u32[]{:S(2)}) %copy-start.2) | copy-done | bytes 278552
  9.4 0.0 copy-start.6
  9.4 0.6 %copy-done.6 = f32[4,24,128]{2,1,0:T(8,128)} copy-done((f32[4,24,128]{2,1,0:T(8,128)}, f32[4,24,128]{2,1,0:T(8,128)S(1)}, u32[]{:S(2)}) %copy-start.6) | copy-done | bytes 49176
  10.0 0.0 copy-start.1
  10.0 15.7 %exchange.1 = (f32[4,136,128]{2,1,0:T(8,128)}, f32[4,24,128]{2,1,0:T(8,128)}) custom-call(f32[4,136,128]{2,1,0:T(8,128)} %copy-done.2, f32[4,24,128]{2,1,0:T(8,128)} %copy-done.6), custom_call_target="tpu_custom_call" | custom-call | tf_op jit(solution)/shard_map/exchange/pallas_call | solution.py:378
  25.7 0.0 copy-done.1
  25.7 0.0 copy-start.3
  25.7 0.9 %copy-done.3 = f32[4,136,128]{2,1,0:T(8,128)S(1)} copy-done((f32[4,136,128]{2,1,0:T(8,128)S(1)}, f32[4,136,128]{2,1,0:T(8,128)}, u32[]{:S(2)}) %copy-start.3) | copy-done | bytes 278552
  26.7 0.0 copy-start.5
  26.7 0.8 %copy-done.5 = f32[4,24,128]{2,1,0:T(8,128)S(1)} copy-done((f32[4,24,128]{2,1,0:T(8,128)S(1)}, f32[4,24,128]{2,1,0:T(8,128)}, u32[]{:S(2)}) %copy-start.5) | copy-done | bytes 49176
  27.5 6.8 %collide.1 = (f32[3,96,128]{2,1,0:T(8,128)}, f32[3,64,128]{2,1,0:T(8,128)}) custom-call(s32[4]{0:T(128)S(1)} %bitcast.11, s32[3]{0:T(128)S(1)} %copy-done.9, f32[3,64,128]{2,1,0:T(8,128)S(1)} %bitcast.7, f32[64,128]{1,0:T(8,128)S(1)} %get-tuple-element.10.ids, f32[10,56,128]{2,1,0:T(8,128)S(1)} %get-tuple-element.11.grid, f32[4,136,128]{2,1,0:T(8,128)S(1)} %copy-done.3, ...), custom_call_target="tpu_custom_call" | custom-call | tf_op jit(solution)/shard_map/collide/pallas_call | solution.py:387
Async XLA Ops:
  0.6 0.7 %copy-start.8 = (s32[1,1,4]{2,1,0:T(1,128)S(1)}, s32[1,1,4]{2,1,0:T(1,128)}, u32[]{:S(2)}) copy-start(s32[1,1,4]{2,1,0:T(1,128)} %param.7) | copy-start | bytes 52
  0.6 0.7 %copy-start.9 = (s32[3]{0:T(128)S(1)}, s32[3]{0:T(128)}, u32[]{:S(2)}) copy-start(s32[3]{0:T(128)} %shift.3) | copy-start | bytes 40
  1.3 0.9 %copy-start = (f32[3,1,1,8192]{3,2,1,0:T(1,128)S(1)}, f32[3,1,1,8192]{3,2,1,0:T(1,128)}, u32[]{:S(2)}) copy-start(f32[3,1,1,8192]{3,2,1,0:T(1,128)} %param.5) | copy-start | bytes 294916
  2.2 0.9 %copy-start.4 = (f32[3,1,1,8192]{3,2,1,0:T(1,128)S(1)}, f32[3,1,1,8192]{3,2,1,0:T(1,128)}, u32[]{:S(2)}) copy-start(f32[3,1,1,8192]{3,2,1,0:T(1,128)} %param.6) | copy-start | bytes 294916
  3.1 0.8 %copy-start.7 = (s32[1,1,8192]{2,1,0:T(1,128)S(1)}, s32[1,1,8192]{2,1,0:T(1,128)}, u32[]{:S(2)}) copy-start(s32[1,1,8192]{2,1,0:T(1,128)} %param.9) | copy-start | bytes 98308
  8.7 0.7 %copy-start.2 = (f32[4,136,128]{2,1,0:T(8,128)}, f32[4,136,128]{2,1,0:T(8,128)S(1)}, u32[]{:S(2)}) copy-start(f32[4,136,128]{2,1,0:T(8,128)S(1)} %get-tuple-element.12.side) | copy-start | bytes 835588
  9.4 0.6 %copy-start.6 = (f32[4,24,128]{2,1,0:T(8,128)}, f32[4,24,128]{2,1,0:T(8,128)S(1)}, u32[]{:S(2)}) copy-start(f32[4,24,128]{2,1,0:T(8,128)S(1)} %get-tuple-element.13.corner) | copy-start | bytes 147460
  10.0 15.7 %copy-start.1 = (f32[3,1,1,8192]{3,2,1,0:T(1,128)S(1)}, f32[3,1,1,8192]{3,2,1,0:T(1,128)}, u32[]{:S(2)}) copy-start(f32[3,1,1,8192]{3,2,1,0:T(1,128)} %param.5) | copy-start | bytes 294916
  25.7 1.0 %copy-start.3 = (f32[4,136,128]{2,1,0:T(8,128)S(1)}, f32[4,136,128]{2,1,0:T(8,128)}, u32[]{:S(2)}) copy-start(f32[4,136,128]{2,1,0:T(8,128)} %get-tuple-element.14.side) | copy-start | bytes 835588
  26.7 0.8 %copy-start.5 = (f32[4,24,128]{2,1,0:T(8,128)S(1)}, f32[4,24,128]{2,1,0:T(8,128)}, u32[]{:S(2)}) copy-start(f32[4,24,128]{2,1,0:T(8,128)} %get-tuple-element.15.corner) | copy-start | bytes 147460

commit v2 on v1

v2 whole, which is shorter than its diff:
```python
import math

import jax
import jax.numpy as jnp
from jax import lax
from jax.experimental import pallas as pl
from jax.experimental.pallas import tpu as pltpu
from jax.sharding import PartitionSpec as P

CXL = 8
CYL = 8
CZ = 128
NAX = 16
MIG = 1024
ROWS = 64
SLOTS = 96
GRID = 10
HALF = GRID // 2
CELL_ROWS = GRID * HALF
PAD_ROWS = 56
PLANES = 10

COS_TURN = -0.6427876096865393
SIN_TURN = 0.766044443118978
GOLDEN_TURN = 2.399963229728653

F32 = jnp.float32
BF16 = jnp.bfloat16
MESH = pl.DeviceIdType.MESH


def axis_table():
    table = []
    for number in range(NAX):
        height = 1.0 - (2.0 * number + 1.0) / NAX
        radius = math.sqrt(1.0 - height * height)
        phase = number * GOLDEN_TURN
        table.append((radius * math.cos(phase), radius * math.sin(phase), height))
    return table


def split(value):
    high = value.astype(BF16)
    return high, (value - high.astype(F32)).astype(BF16)


def dot_nt(a, b):
    return lax.dot_general(a, b, (((1,), (1,)), ((), ())), preferred_element_type=F32)


def iota(shape, dim):
    return lax.broadcasted_iota(jnp.int32, shape, dim)


def neighbours():
    x, y = lax.axis_index("gx"), lax.axis_index("gy")
    nx, ny = lax.axis_size("gx"), lax.axis_size("gy")
    left, right = lax.rem(x + nx - 1, nx), lax.rem(x + 1, nx)
    down, up = lax.rem(y + ny - 1, ny), lax.rem(y + 1, ny)
    sides = [(left, y), (right, y), (x, down), (x, up)]
    corners = [(left, down), (left, up), (right, down), (right, up)]
    return sides + corners


def strips(load, side, corner, planes):
    for p in range(planes):
        at = slice(p * 10, p * 10 + 10)
        side[0, at, :] = load(p, 0, 10, 1)
        side[1, at, :] = load(p, 40, 10, 1)
        side[2, at, :] = load(p, 0, 10, 5)
        side[3, at, :] = load(p, 4, 10, 5)
        for k, start in enumerate((0, 4, 40, 44)):
            corner[k, p * 2 : p * 2 + 2, :] = load(p, start, 2, 5)


def prep_kernel(
    leaving_in, shift_in, vel_in, pos_in, axis_in,
    grid, own_axis, ids, got_axis, got_axis_c, got_sum, got_sum_c, got_run, got_run_c,
    leaving, shift, vel, pos, axis, row_s, col_s, sums, run_s, prep_s, axis_s,
    axis_o, axis_oc, sum_o, sum_oc, run_o, run_oc, load_sem, send_sem, recv_sem,
):
    loads = [
        pltpu.make_async_copy(source, target, load_sem.at[k])
        for k, (source, target) in enumerate(
            ((pos_in, pos), (shift_in, shift), (axis_in, axis), (vel_in, vel), (leaving_in, leaving))
        )
    ]
    for load in loads:
        load.start()
    targets = neighbours()
    barrier = pltpu.get_barrier_semaphore()
    for target in targets:
        pl.semaphore_signal(barrier, inc=1, device_id=target, device_id_type=MESH)

    sent = []

    def send(kind, side, corner, got, got_c):
        for k in range(8):
            source, target = (side.at[k], got.at[k]) if k < 4 else (corner.at[k - 4], got_c.at[k - 4])
            copy = pltpu.make_async_remote_copy(
                src_ref=source,
                dst_ref=target,
                send_sem=send_sem.at[kind, k],
                recv_sem=recv_sem.at[kind, k],
                device_id=targets[k],
                device_id_type=MESH,
            )
            copy.start()
            sent.append(copy)

    axis_s[...] = jnp.zeros(axis_s.shape, F32)
    axis_o[:, 16:24, :] = jnp.zeros((4, 8, 128), F32)
    axis_oc[...] = jnp.zeros((4, 8, 128), F32)
    loads[2].wait()
    for cx in range(CXL):
        base = 5 + cx * HALF
        even = axis[pl.ds(cx * 8, 4, stride=2), :].astype(F32)
        odd = axis[pl.ds(cx * 8 + 1, 4, stride=2), :].astype(F32)
        axis_s[0, base : base + 4, :] = even
        axis_s[1, base + 1 : base + 5, :] = odd
        axis_s[2, base : base + 4, :] = odd
        axis_s[3, base : base + 4, :] = even
    loads[1].wait()
    low_x = (shift[0] == 1).astype(jnp.int32)
    low_y = (shift[1] == 1).astype(jnp.int32)
    for par in range(2):
        own_axis[par] = axis_s[2 * par + low_y, pl.ds(5 - 5 * low_x, PAD_ROWS), :]
    strips(lambda p, at, n, step: own_axis[p, pl.ds(at, n, stride=step), :], axis_o, axis_oc, 2)
    pl.semaphore_wait(barrier, 8)
    send(0, axis_o, axis_oc, got_axis, got_axis_c)

    loads[0].wait()
    shifts = [shift[k].astype(F32) * 0.25 for k in range(3)]
    cell_x = jnp.floor(pos[0] + shifts[0]) + low_x.astype(F32)
    cell_y = jnp.floor(pos[1] + shifts[1]) + low_y.astype(F32)
    cell_z = jnp.floor(pos[2] + shifts[2])
    cell_z = jnp.where(cell_z >= float(CZ), cell_z - float(CZ), cell_z)
    half = jnp.floor(cell_y * 0.5)
    row = cell_x * float(HALF) + half
    col = (cell_y - 2.0 * half) * float(CZ) + cell_z
    row_s[...] = row
    col_s[...] = col
    ids[...] = row * 256.0 + col

    loads[3].wait()
    row_of = iota((64, 128), 0).astype(F32).astype(BF16)
    col_of = iota((256, 128), 0).astype(F32).astype(BF16)
    zero = jnp.zeros((64, 128), BF16)
    one = jnp.ones((64, 128), BF16)
    for chunk in range(8):
        left_parts = [[] for _ in range(7)]
        right_parts = []
        for j in range(8):
            r = chunk * 8 + j
            hit = row_of == jnp.broadcast_to(row_s[r : r + 1, :], (64, 128)).astype(BF16)
            left_parts[0].append(jnp.where(hit, one, zero))
            for c in range(3):
                high, low = split(vel[c, r : r + 1, :])
                high = jnp.broadcast_to(high.astype(F32), (64, 128)).astype(BF16)
                low = jnp.broadcast_to(low.astype(F32), (64, 128)).astype(BF16)
                left_parts[1 + 2 * c].append(jnp.where(hit, high, zero))
                left_parts[2 + 2 * c].append(jnp.where(hit, low, zero))
            hit = col_of == jnp.broadcast_to(col_s[r : r + 1, :], (256, 128)).astype(BF16)
            right_parts.append(
                jnp.where(hit, jnp.ones((256, 128), BF16), jnp.zeros((256, 128), BF16))
            )
        part = dot_nt(
            jnp.concatenate([jnp.concatenate(p, 1) for p in left_parts], 0),
            jnp.concatenate(right_parts, 1),
        )
        if chunk == 0:
            sums[...] = part
        else:
            sums[...] += part
    for par in range(2):
        lanes = slice(par * 128, (par + 1) * 128)
        grid[par] = sums[0:PAD_ROWS, lanes]
        for c in range(3):
            at = 64 + 128 * c
            grid[2 + 2 * c + par] = sums[at : at + PAD_ROWS, lanes] + sums[at + 64 : at + 64 + PAD_ROWS, lanes]
    strips(lambda p, at, n, step: grid[p, pl.ds(at, n, stride=step), :], sum_o, sum_oc, 8)
    send(1, sum_o, sum_oc, got_sum, got_sum_c)

    loads[4].wait()
    slot = iota((8, 128), 0) * 128 + iota((8, 128), 1)
    lane = iota((8, 128), 1)
    counts = [leaving[k] for k in range(4)]
    starts = [jnp.int32(0), counts[0], counts[0] + counts[1], counts[0] + counts[1] + counts[2]]

    def run(load, d):
        if d == 0:
            return load(0)
        q = starts[d] // 128
        r = starts[d] - q * 128
        back = jnp.where(r == 0, 0, 128 - r)
        here = pltpu.roll(load(q), back, 1)
        after = pltpu.roll(load(q + 1), back, 1)
        return jnp.where(lane < 128 - r, here, after)

    moves = (40.0, -40.0, 4.0, -4.0)
    flags = []
    for d in range(4):
        live = slot < counts[d]
        values = [run(lambda q, c=c: vel[c, pl.ds(q, 8), :], d) for c in range(3)]
        run_id = run(lambda q: ids[pl.ds(q, 8), :], d)
        kept = live
        if d < 2:
            y = run(lambda q: pos[1, pl.ds(q, 8), :], d)
            down = live & (y < 0.0)
            up = live & (y >= float(CYL))
            kept = live & (y >= 0.0) & (y < float(CYL))
            flags += [down, up]
            for c in range(3):
                high = values[c].astype(BF16).astype(F32)
                run_s[d, 16 * c : 16 * c + 8, :] = high
                run_s[d, 16 * c + 8 : 16 * c + 16, :] = values[c] - high
            run_row = jnp.floor(run_id * (1.0 / 256.0))
            run_s[d, 48:56, :] = run_row
            run_s[d, 56:64, :] = run_id - run_row * 256.0
            run_s[d, 64:72, :] = jnp.ones((8, 128), F32)
            run_s[d, 72:128, :] = jnp.zeros((56, 128), F32)
        for c in range(3):
            run_o[d, 8 * c : 8 * c + 8, :] = values[c]
        run_o[d, 24:32, :] = jnp.where(kept, run_id + moves[d] * 256.0, -1.0)

    flag = jnp.concatenate([f.astype(F32) for f in flags], 0)
    flag16 = flag.astype(BF16)
    before = (iota((128, 128), 0) < iota((128, 128), 1)).astype(F32).astype(BF16)
    inside = jnp.dot(flag16, before, preferred_element_type=F32)
    total = jnp.dot(flag16, jnp.ones((128, 128), BF16), preferred_element_type=F32)
    r0, r1 = iota((32, 32), 0), iota((32, 32), 1)
    earlier = ((r1 < r0) & (r0 // 8 == r1 // 8)).astype(F32).astype(BF16)
    offset = jnp.dot(earlier, total.astype(BF16), preferred_element_type=F32)
    rank = jnp.where(flag > 0.0, inside + offset, -1.0)
    prep_s[...] = rank
    rank_of = iota((128, 128), 0).astype(F32).astype(BF16)
    for d in range(2):
        rows = jnp.concatenate(
            [run_s[d, pl.ds(r, 16, stride=8), :] for r in range(8)], 1
        ).astype(BF16)
        for s in range(2):
            at = d * 16 + s * 8
            hits = []
            for r in range(8):
                hit = rank_of == jnp.broadcast_to(prep_s[at + r : at + r + 1, :], (128, 128)).astype(BF16)
                hits.append(jnp.where(hit, jnp.ones((128, 128), BF16), jnp.zeros((128, 128), BF16)))
            packed = dot_nt(rows, jnp.concatenate(hits, 1))
            k = d * 2 + s
            for c in range(3):
                run_oc[k, c : c + 1, :] = packed[2 * c : 2 * c + 1] + packed[2 * c + 1 : 2 * c + 2]
            moved = packed[6:7] * 256.0 + packed[7:8] + (moves[d] + moves[2 + s]) * 256.0
            run_oc[k, 3:4, :] = jnp.where(packed[8:9] > 0.5, moved, -1.0)
            run_oc[k, 4:8, :] = jnp.zeros((4, 128), F32)
    send(2, run_o, run_oc, got_run, got_run_c)
    for copy in sent:
        copy.wait()


def collide_kernel(
    leaving_in, shift_in, vel_in, ids, grid, own_axis, got_axis, got_axis_c, got_sum, got_sum_c, got_run, got_run_c,
    out_hbm, flow_hbm,
    leaving, shift, slot_v, out, flow, total, slot_id, load_sem, store_sem,
):
    loads = [
        pltpu.make_async_copy(source, target, load_sem.at[k])
        for k, (source, target) in enumerate(
            ((shift_in, shift), (leaving_in, leaving), (vel_in, slot_v.at[:, 0:ROWS, :]))
        )
    ]
    for load in loads:
        load.start()
    for p in range(PLANES):
        if p < 8:
            own, side, corner, q = grid, got_sum, got_sum_c, p
        else:
            own, side, corner, q = own_axis, got_axis, got_axis_c, p - 8
        total[p] = own[q]
        at = slice(q * 10, q * 10 + 10)
        total[p, 0:10, :] += side[1, at, :]
        total[p, 40:50, :] += side[0, at, :]
        total[p, pl.ds(0, 10, stride=5), :] += side[3, at, :]
        total[p, pl.ds(4, 10, stride=5), :] += side[2, at, :]
        for k, start in ((3, 0), (2, 4), (1, 40), (0, 44)):
            total[p, pl.ds(start, 2, stride=5), :] += corner[k, q * 2 : q * 2 + 2, :]
    high_rows = [[], [], [], []]
    low_rows = [[], [], []]
    most = [jnp.maximum(total[par], 1.0) for par in range(2)]
    for c in range(3):
        means = [total[2 + 2 * c + par] / most[par] for par in range(2)]
        for par in range(2):
            total[2 + 2 * c + par] = means[par]
        mean = jnp.concatenate(means, 1)
        high = mean.astype(BF16).astype(F32)
        high_rows[c] = high
        low_rows[c] = mean - high
    high_rows[3] = jnp.concatenate([total[8], total[9]], 1)
    table = jnp.concatenate(high_rows + low_rows + [jnp.zeros((8, 256), F32)], 0).astype(BF16)

    loads[0].wait()
    low_x = (shift[0] == 1).astype(jnp.int32)
    low_y = (shift[1] == 1).astype(jnp.int32)
    for cx in range(CXL):
        base = (cx + low_x) * HALF
        for c in range(3):
            flow[c, pl.ds(cx * 8, 4, stride=2), :] = total[2 + 2 * c + low_y, pl.ds(base, 4), :]
            flow[c, pl.ds(cx * 8 + 1, 4, stride=2), :] = total[
                3 + 2 * c - low_y, pl.ds(base + low_y, 4), :
            ]
    stores = [pltpu.make_async_copy(flow, flow_hbm, store_sem.at[0])]
    stores[0].start()

    loads[1].wait()
    loads[2].wait()
    slot = iota((8, 128), 0) * 128 + iota((8, 128), 1)
    for c in range(3):
        slot_v[c, 64:72, :] = got_run[1, 8 * c : 8 * c + 8, :]
        slot_v[c, 72:80, :] = got_run[0, 8 * c : 8 * c + 8, :]
    gone = leaving[0] + leaving[1] + leaving[2] + leaving[3]
    place = iota((ROWS, 128), 0) * 128 + iota((ROWS, 128), 1)
    slot_id[0:ROWS, :] = jnp.where(place >= gone, ids[...], -1.0)
    slot_id[64:72, :] = got_run[1, 24:32, :]
    slot_id[72:80, :] = got_run[0, 24:32, :]
    for at, d, first, second in ((80, 3, 3, 1), (88, 2, 2, 0)):
        run_id = got_run[d, 24:32, :]
        n0 = jnp.sum((run_id >= 0.0).astype(jnp.int32))
        n1 = jnp.sum((got_run_c[first, 3:4, :] >= 0.0).astype(jnp.int32))
        in_first = (slot >= n0) & (slot < n0 + n1)
        in_second = (slot >= n0 + n1) & (slot < n0 + n1 + 128)
        turn = lax.rem(n0, 128)
        turn2 = lax.rem(n0 + n1, 128)
        for c in range(4):
            one = pltpu.roll(jnp.broadcast_to(got_run_c[first, c : c + 1, :], (8, 128)), turn, 1)
            two = pltpu.roll(jnp.broadcast_to(got_run_c[second, c : c + 1, :], (8, 128)), turn2, 1)
            base = got_run[d, 8 * c : 8 * c + 8, :]
            merged = jnp.where(in_first, one, jnp.where(in_second, two, base))
            if c < 3:
                slot_v[c, at : at + 8, :] = merged
            else:
                slot_id[at : at + 8, :] = merged

    col_of = iota((256, 128), 0).astype(F32).astype(BF16)
    row_of = iota((PAD_ROWS, 128), 0).astype(F32)
    out[:, 0:8, :] = jnp.zeros((3, 8, 128), F32)
    choices = axis_table()
    for b in range(11):
        at = slice(8 + b * 8, 16 + b * 8)
        block = slot_id[at, :]
        rows = jnp.floor(block * (1.0 / 256.0))
        cols = block - rows * 256.0
        looked = [[], [], [], []]
        for j in range(0, 8, 2):
            hits = []
            for i in (j, j + 1):
                hit = col_of == jnp.broadcast_to(cols[i : i + 1, :], (256, 128)).astype(BF16)
                hits.append(jnp.where(hit, jnp.ones((256, 128), BF16), jnp.zeros((256, 128), BF16)))
            both = jnp.dot(table, jnp.concatenate(hits, 1), preferred_element_type=F32)
            for i in (0, 1):
                lanes = slice(i * 128, i * 128 + 128)
                hit = row_of == jnp.broadcast_to(rows[j + i : j + i + 1, :], (PAD_ROWS, 128))
                for c in range(4):
                    part = both[PAD_ROWS * c : PAD_ROWS * (c + 1), lanes]
                    if c < 3:
                        part = part + both[PAD_ROWS * (4 + c) : PAD_ROWS * (5 + c), lanes]
                    looked[c].append(jnp.sum(jnp.where(hit, part, 0.0), axis=0, keepdims=True))
        mean = [jnp.concatenate(looked[c], 0) for c in range(3)]
        number = jnp.concatenate(looked[3], 0).astype(jnp.int32)
        bits = [(number & (1 << k)) != 0 for k in range(4)]
        a = []
        for c in range(3):
            level = [entry[c] for entry in choices]
            for k in range(4):
                level = [
                    jnp.where(bits[k], level[2 * m + 1], level[2 * m]) for m in range(len(level) // 2)
                ]
            a.append(level[0])
        live = block >= 0.0
        w = [slot_v[c, at, :] - mean[c] for c in range(3)]
        cross = [
            a[1] * w[2] - a[2] * w[1],
            a[2] * w[0] - a[0] * w[2],
            a[0] * w[1] - a[1] * w[0],
        ]
        along = (a[0] * w[0] + a[1] * w[1] + a[2] * w[2]) * (1.0 - COS_TURN)
        for c in range(3):
            turned = mean[c] + COS_TURN * w[c] + SIN_TURN * cross[c] + along * a[c]
            out[c, at, :] = jnp.where(live, turned, 0.0)
    stores.append(pltpu.make_async_copy(out, out_hbm, store_sem.at[1]))
    stores[1].start()
    for store in stores:
        store.wait()


def shape(*dims):
    return jax.ShapeDtypeStruct(dims, F32)


def per_device(velocity, position, leaving, grid_shift, axis_index):
    vel = velocity.reshape(3, ROWS, 128)
    pos = position.reshape(3, ROWS, 128)
    axis = axis_index.reshape(64, 128)
    leaving = leaving.reshape(4)
    vmem = pl.BlockSpec(memory_space=pltpu.VMEM)
    anywhere = pl.BlockSpec(memory_space=pl.ANY)
    parts = pl.pallas_call(
        prep_kernel,
        name="prep",
        out_shape=(
            shape(8, PAD_ROWS, 128),
            shape(2, PAD_ROWS, 128),
            shape(ROWS, 128),
            shape(4, 24, 128),
            shape(4, 8, 128),
            shape(4, 80, 128),
            shape(4, 16, 128),
            shape(4, 32, 128),
            shape(4, 8, 128),
        ),
        in_specs=[anywhere] * 5,
        out_specs=(vmem,) * 9,
        scratch_shapes=[
            pltpu.SMEM((4,), jnp.int32),
            pltpu.SMEM((3,), jnp.int32),
            pltpu.VMEM((3, ROWS, 128), F32),
            pltpu.VMEM((3, ROWS, 128), F32),
            pltpu.VMEM((64, 128), jnp.int32),
            pltpu.VMEM((ROWS, 128), F32),
            pltpu.VMEM((ROWS, 128), F32),
            pltpu.VMEM((448, 256), F32),
            pltpu.VMEM((2, 128, 128), F32),
            pltpu.VMEM((32, 128), F32),
            pltpu.VMEM((4, 64, 128), F32),
            pltpu.VMEM((4, 24, 128), F32),
            pltpu.VMEM((4, 8, 128), F32),
            pltpu.VMEM((4, 80, 128), F32),
            pltpu.VMEM((4, 16, 128), F32),
            pltpu.VMEM((4, 32, 128), F32),
            pltpu.VMEM((4, 8, 128), F32),
            pltpu.SemaphoreType.DMA((5,)),
            pltpu.SemaphoreType.DMA((3, 8)),
            pltpu.SemaphoreType.DMA((3, 8)),
        ],
        compiler_params=pltpu.CompilerParams(
            collective_id=0, has_side_effects=True, vmem_limit_bytes=32 << 20
        ),
    )(leaving, grid_shift, vel, pos, axis)
    grid, own_axis, ids = parts[:3]
    out, flow = pl.pallas_call(
        collide_kernel,
        name="collide",
        out_shape=(shape(3, SLOTS, 128), shape(3, 64, 128)),
        in_specs=[anywhere] * 3 + [vmem] * 9,
        out_specs=(anywhere, anywhere),
        scratch_shapes=[
            pltpu.SMEM((4,), jnp.int32),
            pltpu.SMEM((3,), jnp.int32),
            pltpu.VMEM((3, SLOTS, 128), F32),
            pltpu.VMEM((3, SLOTS, 128), F32),
            pltpu.VMEM((3, 64, 128), F32),
            pltpu.VMEM((PLANES, PAD_ROWS, 128), F32),
            pltpu.VMEM((SLOTS, 128), F32),
            pltpu.SemaphoreType.DMA((3,)),
            pltpu.SemaphoreType.DMA((2,)),
        ],
        compiler_params=pltpu.CompilerParams(vmem_limit_bytes=32 << 20),
    )(leaving, grid_shift, vel, ids, grid, own_axis, *parts[3:])
    return out.reshape(3, 1, 1, SLOTS * 128), flow.reshape(3, 1, 1, 64 * 128)


def solution(mesh):
    return jax.shard_map(
        per_device,
        mesh=mesh,
        in_specs=(
            P(None, "gx", "gy", None),
            P(None, "gx", "gy", None),
            P("gx", "gy", None),
            P(),
            P("gx", "gy", None),
        ),
        out_specs=(P(None, "gx", "gy", None), P(None, "gx", "gy", None)),
        check_vma=False,
    )
```

time: 34.6 us -> 26.8 us (0.77)
  Pallas kernels: 27.3 us -> 22.8 us
  local copies, waits for them, and re-layouts: 6.28 us -> 3.2 us
    pallas_call x3 -> x2, Pallas kernels: 27.3 us -> 22.8 us  [the longest x1 18.8 us: per_device(): pl.pallas_call(prep_kernel, name='prep', out_shape=(shape(8, PAD_ROWS, 12...]
    unnamed x20 -> x10, local copies, waits for them, and re-layouts: 6.28 us -> 3.2 us
where the time goes in v2:
time: 26.8 us; the launch traced here: 26.6 us
  Pallas kernels  22.8 us (85%)
  local copies, waits for them, and re-layouts  3.2 us (12%)
  between operations  0.66 us (2%)
    pallas_call x1, Pallas kernels, per_device(): pl.pallas_call(prep_kernel, name='prep', out_shape=(shape(8, PAD_ROWS, 12...  18.8 us
    pallas_call x1, Pallas kernels, per_device(): pl.pallas_call(collide_kernel, name='collide', out_shape=(shape(3, SLOTS,...  3.98 us
    unnamed x10, local copies, waits for them, and re-layouts  3.2 us

profile of v2, /device:TPU:1, one launch (start us, length us, event | category | flops | bytes accessed | tf_op | source)
XLA Modules:
  0.0 26.6 jit_solution(13897504375833119194)
XLA Ops:
  0.6 0.0 copy-start.3
  0.6 0.0 copy-start.4
  0.7 0.6 %copy-done.3 = s32[1,1,4]{2,1,0:T(1,128)S(1)} copy-done((s32[1,1,4]{2,1,0:T(1,128)S(1)}, s32[1,1,4]{2,1,0:T(1,128)}, u32[]{:S(2)}) %copy-start.3) | copy-done | bytes 40
  1.3 0.0 copy-done.4
  1.3 0.0 copy-start
  1.3 0.9 %copy-done = f32[3,1,1,8192]{3,2,1,0:T(1,128)S(1)} copy-done((f32[3,1,1,8192]{3,2,1,0:T(1,128)S(1)}, f32[3,1,1,8192]{3,2,1,0:T(1,128)}, u32[]{:S(2)}) %copy-start) | copy-done | bytes 98328
  2.2 0.0 copy-start.1
  2.2 0.9 %copy-done.1 = f32[3,1,1,8192]{3,2,1,0:T(1,128)S(1)} copy-done((f32[3,1,1,8192]{3,2,1,0:T(1,128)S(1)}, f32[3,1,1,8192]{3,2,1,0:T(1,128)}, u32[]{:S(2)}) %copy-start.1) | copy-done | bytes 98328
  3.1 0.0 copy-start.2
  3.1 0.8 %copy-done.2 = s32[1,1,8192]{2,1,0:T(1,128)S(1)} copy-done((s32[1,1,8192]{2,1,0:T(1,128)S(1)}, s32[1,1,8192]{2,1,0:T(1,128)}, u32[]{:S(2)}) %copy-start.2) | copy-done | bytes 32792
  3.8 18.8 %prep.1 = (f32[8,56,128]{2,1,0:T(8,128)S(1)}, f32[2,56,128]{2,1,0:T(8,128)S(1)}, f32[64,128]{1,0:T(8,128)S(1)}, f32[4,24,128]{2,1,0:T(8,128)S(1)}, f32[4,8,128]{...) custom-call(s32[4]{0:T(128)S(1)} %bitcast.10, ...), custom_call_target="tpu_custom_call" | custom-call | tf_op jit(solution)/shard_map/prep/pallas_call | solution.py:404
  22.6 4.0 %collide.1 = (f32[3,96,128]{2,1,0:T(8,128)}, f32[3,64,128]{2,1,0:T(8,128)}) custom-call(s32[4]{0:T(128)S(1)} %bitcast.11, s32[3]{0:T(128)S(1)} %copy-done.4, f32[3,64,128]{2,1,0:T(8,128)S(1)} %bitcast.7, f32[64,128]{1,0:T(8,128)S(1)} %get-tuple-element.13.ids, f32[8,56,128]{2,1,0:T(8,128)S(1)} %get-tuple-element.14.grid, ...), custom_call_target="tpu_custom_call" | custom-call | tf_op jit(solution)/shard_map/collide/pallas_call | solution.py:447
Async XLA Ops:
  0.6 0.7 %copy-start.3 = (s32[1,1,4]{2,1,0:T(1,128)S(1)}, s32[1,1,4]{2,1,0:T(1,128)}, u32[]{:S(2)}) copy-start(s32[1,1,4]{2,1,0:T(1,128)} %param.7) | copy-start | bytes 52
  0.6 0.7 %copy-start.4 = (s32[3]{0:T(128)S(1)}, s32[3]{0:T(128)}, u32[]{:S(2)}) copy-start(s32[3]{0:T(128)} %shift_in.3) | copy-start | bytes 40
  1.3 0.9 %copy-start = (f32[3,1,1,8192]{3,2,1,0:T(1,128)S(1)}, f32[3,1,1,8192]{3,2,1,0:T(1,128)}, u32[]{:S(2)}) copy-start(f32[3,1,1,8192]{3,2,1,0:T(1,128)} %param.5) | copy-start | bytes 294916
  2.2 0.9 %copy-start.1 = (f32[3,1,1,8192]{3,2,1,0:T(1,128)S(1)}, f32[3,1,1,8192]{3,2,1,0:T(1,128)}, u32[]{:S(2)}) copy-start(f32[3,1,1,8192]{3,2,1,0:T(1,128)} %param.6) | copy-start | bytes 294916
  3.1 0.8 %copy-start.2 = (s32[1,1,8192]{2,1,0:T(1,128)S(1)}, s32[1,1,8192]{2,1,0:T(1,128)}, u32[]{:S(2)}) copy-start(s32[1,1,8192]{2,1,0:T(1,128)} %param.9) | copy-start | bytes 98308

commit v3 on v2

--- a/solution.py
+++ b/solution.py
@@ -126,8 +126,6 @@
     for par in range(2):
         own_axis[par] = axis_s[2 * par + low_y, pl.ds(5 - 5 * low_x, PAD_ROWS), :]
     strips(lambda p, at, n, step: own_axis[p, pl.ds(at, n, stride=step), :], axis_o, axis_oc, 2)
-    pl.semaphore_wait(barrier, 8)
-    send(0, axis_o, axis_oc, got_axis, got_axis_c)
 
     loads[0].wait()
     shifts = [shift[k].astype(F32) * 0.25 for k in range(3)]
@@ -179,7 +177,9 @@
             at = 64 + 128 * c
             grid[2 + 2 * c + par] = sums[at : at + PAD_ROWS, lanes] + sums[at + 64 : at + 64 + PAD_ROWS, lanes]
     strips(lambda p, at, n, step: grid[p, pl.ds(at, n, stride=step), :], sum_o, sum_oc, 8)
+    pl.semaphore_wait(barrier, 8)
     send(1, sum_o, sum_oc, got_sum, got_sum_c)
+    send(0, axis_o, axis_oc, got_axis, got_axis_c)
 
     loads[4].wait()
     slot = iota((8, 128), 0) * 128 + iota((8, 128), 1)
@@ -399,8 +399,11 @@
     pos = position.reshape(3, ROWS, 128)
     axis = axis_index.reshape(64, 128)
     leaving = leaving.reshape(4)
+    vel, pos, axis, leaving, grid_shift = [
+        pltpu.with_memory_space_constraint(v, pltpu.HBM) for v in (vel, pos, axis, leaving, grid_shift)
+    ]
     vmem = pl.BlockSpec(memory_space=pltpu.VMEM)
-    anywhere = pl.BlockSpec(memory_space=pl.ANY)
+    anywhere = pl.BlockSpec(memory_space=pltpu.HBM)
     parts = pl.pallas_call(
         prep_kernel,
         name="prep",

time: 26.8 us -> 21.3 us (0.79)
  local copies, waits for them, and re-layouts: 3.2 us -> 0 us
  Pallas kernels: 22.8 us -> 20.5 us
    unnamed x10 -> x0, local copies, waits for them, and re-layouts: 3.2 us -> none
    pallas_call x1, Pallas kernels: 18.8 us -> 16.2 us  [per_device(): pl.pallas_call(prep_kernel, name='prep', out_shape=(shape(8, PAD_ROWS, 12...]
    pallas_call x1, Pallas kernels: 3.98 us -> 4.29 us  [per_device(): pl.pallas_call(collide_kernel, name='collide', out_shape=(shape(3, SLOTS,...]
where the time goes in v3:
time: 21.3 us; the launch traced here: 21.1 us
  Pallas kernels  20.5 us (96%)
  between operations  0.64 us (3%)
    pallas_call x1, Pallas kernels, per_device(): pl.pallas_call(prep_kernel, name='prep', out_shape=(shape(8, PAD_ROWS, 12...  16.2 us
    pallas_call x1, Pallas kernels, per_device(): pl.pallas_call(collide_kernel, name='collide', out_shape=(shape(3, SLOTS,...  4.29 us

profile of v3, /device:TPU:1, one launch (start us, length us, event | category | flops | bytes accessed | tf_op | source)
XLA Modules:
  0.0 21.1 jit_solution(7165096126589921252)
XLA Ops:
  0.6 16.2 %prep.1 = (f32[8,56,128]{2,1,0:T(8,128)S(1)}, f32[2,56,128]{2,1,0:T(8,128)S(1)}, f32[64,128]{1,0:T(8,128)S(1)}, f32[4,24,128]{2,1,0:T(8,128)S(1)}, f32[4,8,128]{...) custom-call(s32[4]{0:T(128)} %bitcast.10, ...), custom_call_target="tpu_custom_call" | custom-call | tf_op jit(solution)/shard_map/prep/pallas_call | solution.py:407
  16.8 4.3 %collide.1 = (f32[3,96,128]{2,1,0:T(8,128)}, f32[3,64,128]{2,1,0:T(8,128)}) custom-call(s32[4]{0:T(128)} %bitcast.11, s32[3]{0:T(128)} %shift_in.3, f32[3,64,128]{2,1,0:T(8,128)} %bitcast.7, f32[64,128]{1,0:T(8,128)S(1)} %get-tuple-element.13.ids, f32[8,56,128]{2,1,0:T(8,128)S(1)} %get-tuple-element.14.grid, f32[2,56,128]{2,1,0:T(8,128)S(1)} %get-tuple-element.15.own_axis, ...), custom_call_target="tpu_custom_call" | custom-call | tf_op jit(solution)/shard_map/collide/pallas_call | solution.py:450

commit v4 on v3

v4 whole, which is shorter than its diff:
```python
import math

import jax
import jax.numpy as jnp
from jax import lax
from jax.experimental import pallas as pl
from jax.experimental.pallas import tpu as pltpu
from jax.sharding import PartitionSpec as P

CXL = 8
CYL = 8
CZ = 128
NAX = 16
ROWS = 64
SLOTS = 96
BORDER = 32
INNER = 18
MAIN = 48

COS_TURN = -0.6427876096865393
SIN_TURN = 0.766044443118978
GOLDEN_TURN = 2.399963229728653

F32 = jnp.float32
BF16 = jnp.bfloat16
MESH = pl.DeviceIdType.MESH


def axis_table():
    table = []
    for number in range(NAX):
        height = 1.0 - (2.0 * number + 1.0) / NAX
        radius = math.sqrt(1.0 - height * height)
        phase = number * GOLDEN_TURN
        table.append((radius * math.cos(phase), radius * math.sin(phase), height))
    return table


def dot_nt(a, b):
    return lax.dot_general(a, b, (((1,), (1,)), ((), ())), preferred_element_type=F32)


def iota(shape, dim):
    return lax.broadcasted_iota(jnp.int32, shape, dim)


def iota16(shape, dim):
    return iota(shape, dim).astype(F32).astype(BF16)


def spread(row, height):
    return jnp.broadcast_to(row, (height, 128)).astype(BF16)


def one_hot(hit):
    return jnp.where(hit, jnp.ones(hit.shape, BF16), jnp.zeros(hit.shape, BF16))


def high_part(value):
    return value.astype(BF16).astype(F32)


PIECES = (
    [(0, 2, 0, 1, 0, 0), (8, 2, 0, 1, 4, 0), (16, 2, 8, 1, 4, 0), (24, 2, 8, 1, 0, 0)]
    + [(10, 6, 2, 1, 4, 0), (26, 6, 2, 1, 0, 0)]
    + [(2 + 3 * u, 3, u, 0, 1, 1) for u in range(2)]
    + [(18 + 3 * u, 3, 8 + u, 0, 1, 1) for u in range(2)]
    + [(32 + 3 * w, 3, 2 + w, 0, 1, 1) for w in range(6)]
)


def look_up(table, heights, groups, cols, local, j):
    col_of = iota16((256, 128), 0)
    row_of = iota((heights, 128), 0).astype(F32)
    hits = [one_hot(col_of == spread(cols[i : i + 1, :], 256)) for i in (j, j + 1)]
    both = jnp.dot(table, jnp.concatenate(hits, 1), preferred_element_type=F32)
    found = []
    for i in (0, 1):
        lanes = slice(i * 128, i * 128 + 128)
        hit = row_of == jnp.broadcast_to(local[j + i : j + i + 1, :], (heights, 128))
        row = []
        for c in range(4):
            part = both[heights * c : heights * (c + 1), lanes]
            if c < 3:
                part = part + both[heights * (4 + c) : heights * (5 + c), lanes]
            row.append(jnp.sum(jnp.where(hit, part, 0.0), axis=0, keepdims=True))
        found.append(row)
    return found


def look_up_block(table, heights, cols, local):
    found = []
    for j in range(0, 8, 2):
        found += look_up(table, heights, 7, cols, local, j)
    return [jnp.concatenate([row[c] for row in found], 0) for c in range(4)]


def neighbours():
    x, y = lax.axis_index("gx"), lax.axis_index("gy")
    nx, ny = lax.axis_size("gx"), lax.axis_size("gy")
    left, right = lax.rem(x + nx - 1, nx), lax.rem(x + 1, nx)
    down, up = lax.rem(y + ny - 1, ny), lax.rem(y + 1, ny)
    sides = [(left, y), (right, y), (x, down), (x, up)]
    corners = [(left, down), (left, up), (right, down), (right, up)]
    return sides + corners


def prep_kernel(
    leaving_in, shift_in, vel_in, pos_in, axis_in,
    border, own_axis, ids, inner_mean, found, vel, got_sum, got_sum_c, got_run, got_run_c,
    leaving, shift, pos, axis, row_s, col_s, sums, run_s, prep_s, axis_s, run_o, run_oc,
    load_sem, send_sem, recv_sem,
):
    loads = [
        pltpu.make_async_copy(source, target, load_sem.at[k])
        for k, (source, target) in enumerate(
            ((pos_in, pos), (shift_in, shift), (axis_in, axis), (vel_in, vel), (leaving_in, leaving))
        )
    ]
    for load in loads:
        load.start()
    targets = neighbours()
    barrier = pltpu.get_barrier_semaphore()
    for target in targets:
        pl.semaphore_signal(barrier, inc=1, device_id=target, device_id_type=MESH)
    axis_s[...] = jnp.zeros(axis_s.shape, F32)
    run_o[...] = jnp.zeros(run_o.shape, F32)
    for load in loads:
        load.wait()

    low_x = (shift[0] == 1).astype(jnp.int32)
    low_y = (shift[1] == 1).astype(jnp.int32)
    shifts = [shift[k].astype(F32) * 0.25 for k in range(3)]
    cell_x = jnp.floor(pos[0] + shifts[0]) + low_x.astype(F32)
    cell_y = jnp.floor(pos[1] + shifts[1]) + low_y.astype(F32)
    cell_z = jnp.floor(pos[2] + shifts[2])
    cell_z = jnp.where(cell_z >= float(CZ), cell_z - float(CZ), cell_z)
    half = jnp.floor(cell_y * 0.5)
    is_left = cell_x < 2.0
    is_right = cell_x > 7.0
    bottom = cell_x + jnp.where(is_left, 0.0, jnp.where(is_right, 16.0, 24.0))
    middle = 3.0 * cell_x + half + jnp.where(is_left, 1.0, jnp.where(is_right, -7.0, 25.0))
    row = jnp.where(half < 1.0, bottom, jnp.where(half > 3.0, cell_x + 8.0, middle))
    col = (cell_y - 2.0 * half) * float(CZ) + cell_z
    row_s[...] = row
    col_s[...] = col
    ids[...] = row * 256.0 + col

    row_of = iota16((MAIN, 128), 0)
    col_of = iota16((256, 128), 0)
    rest = iota((16, 128), 0)
    rest_row = (MAIN + rest % 2).astype(F32).astype(BF16)
    rest_is = [rest // 2 == g for g in range(7)]
    for chunk in range(8):
        left_parts = [[] for _ in range(8)]
        right_parts = []
        for j in range(8):
            r = chunk * 8 + j
            values = [jnp.ones((1, 128), F32)]
            for c in range(3):
                high = high_part(vel[c, r : r + 1, :])
                values += [high, vel[c, r : r + 1, :] - high]
            hit = row_of == spread(row_s[r : r + 1, :], MAIN)
            tail = jnp.broadcast_to(values[0], (16, 128))
            for g in range(7):
                wide = spread(values[g], MAIN)
                left_parts[g].append(jnp.where(hit, wide, jnp.zeros((MAIN, 128), BF16)))
                if g:
                    tail = jnp.where(rest_is[g], jnp.broadcast_to(values[g], (16, 128)), tail)
            hit = rest_row == spread(row_s[r : r + 1, :], 16)
            left_parts[7].append(jnp.where(hit, tail.astype(BF16), jnp.zeros((16, 128), BF16)))
            right_parts.append(one_hot(col_of == spread(col_s[r : r + 1, :], 256)))
        part = dot_nt(
            jnp.concatenate([jnp.concatenate(p, 1) for p in left_parts], 0),
            jnp.concatenate(right_parts, 1),
        )
        if chunk == 0:
            sums[...] = part
        else:
            sums[...] += part
    for c in range(4):
        if c == 0:
            group = sums[0:BORDER, :]
        else:
            at = (2 * c - 1) * MAIN
            group = sums[at : at + BORDER, :] + sums[at + MAIN : at + MAIN + BORDER, :]
        for par in range(2):
            lanes = slice(par * 128, par * 128 + 128)
            border[pl.ds(2 * c + par, BORDER, stride=8), :] = group[:, lanes]
    border[8 * BORDER : 8 * BORDER + 16, :] = border[0:16, :]

    for cx in range(CXL):
        at = (cx + 1) * 11 + 1
        axis_s[at : at + 8, :] = axis[cx * 8 : cx * 8 + 8, :].astype(F32)
    for par in range(2):
        for first, n, cx, cx_step, half_y, half_step in PIECES:
            start = (cx + 1 - low_x) * 11 + 2 * half_y + par + 1 - low_y
            step = 11 * cx_step + 2 * half_step
            own_axis[par, first : first + n, :] = axis_s[pl.ds(start, n, stride=step), :]
        own_axis[par, 50:56, :] = jnp.zeros((6, 128), F32)
        base = 32 + 16 * par
        for k, order in enumerate(
            (((8, 2), (2, 6), (0, 2)), ((24, 2), (18, 6), (16, 2)), ((0, 2), (26, 6), (24, 2)), ((16, 2), (10, 6), (8, 2)))
        ):
            at = base
            for first, n in order:
                run_o[k, at : at + n, :] = own_axis[par, first : first + n, :]
                at += n
        for k, first in enumerate((0, 8, 24, 16)):
            run_oc[k, 4 + 2 * par : 6 + 2 * par, :] = own_axis[par, first : first + 2, :]

    slot = iota((8, 128), 0) * 128 + iota((8, 128), 1)
    lane = iota((8, 128), 1)
    counts = [leaving[k] for k in range(4)]
    starts = [jnp.int32(0), counts[0], counts[0] + counts[1], counts[0] + counts[1] + counts[2]]

    def run(load, d):
        if d == 0:
            return load(0)
        q = starts[d] // 128
        r = starts[d] - q * 128
        back = jnp.where(r == 0, 0, 128 - r)
        here = pltpu.roll(load(q), back, 1)
        after = pltpu.roll(load(q + 1), back, 1)
        return jnp.where(lane < 128 - r, here, after)

    def moved(d, run_row):
        if d == 0:
            return run_row + jnp.where(run_row < 2.0, 24.0, jnp.where(run_row < 8.0, 16.0, 8.0))
        if d == 1:
            return run_row - jnp.where(run_row < 18.0, 8.0, jnp.where(run_row < 24.0, 16.0, 24.0))
        if d == 2:
            return run_row + jnp.where(run_row < 2.0, 8.0, jnp.where(run_row < 26.0, -8.0, -16.0))
        return run_row + jnp.where(run_row < 10.0, -8.0, jnp.where(run_row < 16.0, 16.0, 8.0))

    flags = []
    for d in range(4):
        live = slot < counts[d]
        values = [run(lambda q, c=c: vel[c, pl.ds(q, 8), :], d) for c in range(3)]
        run_row = run(lambda q: row_s[pl.ds(q, 8), :], d)
        run_col = run(lambda q: col_s[pl.ds(q, 8), :], d)
        kept = live
        if d < 2:
            y = run(lambda q: pos[1, pl.ds(q, 8), :], d)
            down = live & (y < 0.0)
            up = live & (y >= float(CYL))
            kept = live & (y >= 0.0) & (y < float(CYL))
            flags += [down, up]
            for c in range(3):
                high = high_part(values[c])
                run_s[d, 16 * c : 16 * c + 8, :] = high
                run_s[d, 16 * c + 8 : 16 * c + 16, :] = values[c] - high
            run_s[d, 48:56, :] = run_row
            run_s[d, 56:64, :] = run_col
            run_s[d, 64:72, :] = jnp.ones((8, 128), F32)
            run_s[d, 72:128, :] = jnp.zeros((56, 128), F32)
        for c in range(3):
            run_o[d, 8 * c : 8 * c + 8, :] = values[c]
        run_o[d, 24:32, :] = jnp.where(kept, moved(d, run_row) * 256.0 + run_col, -1.0)

    flag = jnp.concatenate([f.astype(F32) for f in flags], 0)
    flag16 = flag.astype(BF16)
    before = (iota((128, 128), 0) < iota((128, 128), 1)).astype(F32).astype(BF16)
    inside = jnp.dot(flag16, before, preferred_element_type=F32)
    total = jnp.dot(flag16, jnp.ones((128, 128), BF16), preferred_element_type=F32)
    r0, r1 = iota((32, 32), 0), iota((32, 32), 1)
    earlier = ((r1 < r0) & (r0 // 8 == r1 // 8)).astype(F32).astype(BF16)
    offset = jnp.dot(earlier, total.astype(BF16), preferred_element_type=F32)
    prep_s[...] = jnp.where(flag > 0.0, inside + offset, -1.0)
    rank_of = iota16((128, 128), 0)
    for d in range(2):
        rows = jnp.concatenate([run_s[d, pl.ds(r, 16, stride=8), :] for r in range(8)], 1).astype(BF16)
        for s in range(2):
            at = d * 16 + s * 8
            hits = [one_hot(rank_of == spread(prep_s[at + r : at + r + 1, :], 128)) for r in range(8)]
            packed = dot_nt(rows, jnp.concatenate(hits, 1))
            k = d * 2 + s
            for c in range(3):
                run_oc[k, c : c + 1, :] = packed[2 * c : 2 * c + 1] + packed[2 * c + 1 : 2 * c + 2]
            there = (packed[6:7] + (16.0 - 32.0 * d)) * 256.0 + packed[7:8]
            run_oc[k, 3:4, :] = jnp.where(packed[8:9] > 0.5, there, -1.0)

    pl.semaphore_wait(barrier, 8)
    copies = []
    for k in (4, 5, 6, 7, 0, 1, 2, 3):
        if k < 4:
            source = border.at[pl.ds(8 * (0, 16, 24, 8)[k], 80), :]
            target = got_sum.at[k]
        else:
            source = border.at[pl.ds(8 * (0, 8, 24, 16)[k - 4], 16), :]
            target = got_sum_c.at[k - 4]
        copies.append((0, k, source, target))
    for k in (4, 5, 6, 7, 0, 1, 2, 3):
        if k < 4:
            copies.append((1, k, run_o.at[k], got_run.at[k]))
        else:
            copies.append((1, k, run_oc.at[k - 4], got_run_c.at[k - 4]))
    sent = []
    for kind, k, source, target in copies:
        copy = pltpu.make_async_remote_copy(
            src_ref=source,
            dst_ref=target,
            send_sem=send_sem.at[kind, k],
            recv_sem=recv_sem.at[kind, k],
            device_id=targets[k],
            device_id_type=MESH,
        )
        copy.start()
        sent.append(copy)

    def inner(group):
        at = group * MAIN + BORDER
        end = 7 * MAIN + 2 * group
        return jnp.concatenate([sums[at : at + 16, :], sums[end : end + 2, :], jnp.zeros((6, 256), F32)], 0)

    most = jnp.maximum(inner(0), 1.0)
    high_rows, low_rows = [], []
    for c in range(3):
        mean = (inner(1 + 2 * c) + inner(2 + 2 * c)) / most
        inner_mean[c] = mean
        high = high_part(mean)
        high_rows.append(high)
        low_rows.append(mean - high)
    high_rows.append(jnp.concatenate([own_axis[0, BORDER:56, :], own_axis[1, BORDER:56, :]], 1))
    table = jnp.concatenate(high_rows + low_rows, 0).astype(BF16)
    for b in range(1, 8):
        at = slice(8 * b, 8 * b + 8)
        looked = look_up_block(table, 24, col_s[at, :], row_s[at, :] - float(BORDER))
        for c in range(4):
            found[c, at, :] = looked[c]
    gone = starts[3] + counts[3]
    place = iota((ROWS, 128), 0) * 128 + iota((ROWS, 128), 1)
    ids[...] = jnp.where(place >= gone, ids[...], -1.0)
    for copy in sent:
        copy.wait()


def collide_kernel(
    shift_in, border, own_axis, ids, inner_mean, found, vel, got_sum, got_sum_c, got_run, got_run_c,
    out_hbm, flow_hbm,
    shift, out, flow, total, means, load_sem, store_sem,
):
    load = pltpu.make_async_copy(shift_in, shift, load_sem)
    load.start()
    total[...] = border[0 : 8 * BORDER, :]
    for k, places in enumerate(
        (
            ((24, 0, 2), (18, 2, 6), (16, 8, 2)),
            ((8, 0, 2), (2, 2, 6), (0, 8, 2)),
            ((16, 0, 2), (10, 2, 6), (8, 8, 2)),
            ((0, 0, 2), (26, 2, 6), (24, 8, 2)),
        )
    ):
        for mine, theirs, n in places:
            total[8 * mine : 8 * (mine + n), :] += got_sum[k, 8 * theirs : 8 * (theirs + n), :]
    for k, mine in enumerate((16, 24, 8, 0)):
        total[8 * mine : 8 * mine + 16, :] += got_sum_c[k]
    numbers = []
    for par in range(2):
        number = own_axis[par, 0:BORDER, :]
        at = 32 + 16 * par
        zero = jnp.zeros((16, 128), F32)
        for k, (before, after) in enumerate(((16, 0), (0, 16), (8, 8))):
            strip = got_run[k, at : at + 16, :]
            parts = [jnp.zeros((before, 128), F32)] * (before > 0) + [strip]
            parts += [jnp.zeros((after, 128), F32)] * (after > 0)
            number = number + jnp.concatenate(parts, 0)
        strip = got_run[3, at : at + 16, :]
        number = number + jnp.concatenate([strip[8:16], zero, strip[0:8]], 0)
        pair = [got_run_c[k, 4 + 2 * par : 6 + 2 * par, :] for k in range(4)]
        gap = jnp.zeros((6, 128), F32)
        number = number + jnp.concatenate([pair[3], gap, pair[2], gap, pair[0], gap, pair[1], gap], 0)
        numbers.append(number)
    groups = [None] * 7
    most = [jnp.maximum(total[pl.ds(par, BORDER, stride=8), :], 1.0) for par in range(2)]
    border_mean = []
    for c in range(3):
        halves = [total[pl.ds(2 + 2 * c + par, BORDER, stride=8), :] / most[par] for par in range(2)]
        mean = jnp.concatenate(halves, 1)
        border_mean.append(mean)
        groups[c] = high_part(mean)
        groups[4 + c] = mean - groups[c]
    groups[3] = jnp.concatenate(numbers, 1)
    table = jnp.concatenate(groups, 0).astype(BF16)
    choices = axis_table()

    def turn(at, live, v, looked):
        mean = looked[:3]
        number = looked[3].astype(jnp.int32)
        bits = [(number & (1 << k)) != 0 for k in range(4)]
        a = []
        for c in range(3):
            level = [entry[c] for entry in choices]
            for k in range(4):
                level = [jnp.where(bits[k], level[2 * m + 1], level[2 * m]) for m in range(len(level) // 2)]
            a.append(level[0])
        w = [v[c] - mean[c] for c in range(3)]
        cross = [
            a[1] * w[2] - a[2] * w[1],
            a[2] * w[0] - a[0] * w[2],
            a[0] * w[1] - a[1] * w[0],
        ]
        along = (a[0] * w[0] + a[1] * w[1] + a[2] * w[2]) * (1.0 - COS_TURN)
        for c in range(3):
            turned = mean[c] + COS_TURN * w[c] + SIN_TURN * cross[c] + along * a[c]
            out[c, at, :] = jnp.where(live, turned, 0.0)

    out[:, 0:8, :] = jnp.zeros((3, 8, 128), F32)
    for b in range(1, 8):
        at = slice(8 * b, 8 * b + 8)
        block = ids[at, :]
        rows = jnp.floor(block * (1.0 / 256.0))
        looked = look_up_block(table, BORDER, block - rows * 256.0, rows)
        turn(at, block >= 0.0, [vel[c, at, :] for c in range(3)], [looked[c] + found[c, at, :] for c in range(4)])

    slot = iota((8, 128), 0) * 128 + iota((8, 128), 1)
    for at, k, window in ((64, 1, 0), (72, 0, 16), (80, 3, 24), (88, 2, 8)):
        v = [got_run[k, 8 * c : 8 * c + 8, :] for c in range(4)]
        if k > 1:
            first, second = ((2, 0), (3, 1))[k - 2]
            n0 = jnp.sum((v[3] >= 0.0).astype(jnp.int32))
            n1 = jnp.sum((got_run_c[first, 3:4, :] >= 0.0).astype(jnp.int32))
            in_first = (slot >= n0) & (slot < n0 + n1)
            in_second = (slot >= n0 + n1) & (slot < n0 + n1 + 128)
            by1, by2 = lax.rem(n0, 128), lax.rem(n0 + n1, 128)
            for c in range(4):
                one = pltpu.roll(jnp.broadcast_to(got_run_c[first, c : c + 1, :], (8, 128)), by1, 1)
                two = pltpu.roll(jnp.broadcast_to(got_run_c[second, c : c + 1, :], (8, 128)), by2, 1)
                v[c] = jnp.where(in_first, one, jnp.where(in_second, two, v[c]))
        rows = jnp.floor(v[3] * (1.0 / 256.0))
        cols = v[3] - rows * 256.0
        if window == 24:
            part = [jnp.concatenate([g[24:32], g[0:8]], 0) for g in groups]
            local = jnp.where(rows < 2.0, rows + 8.0, rows - 24.0)
        else:
            part = [g[window : window + 16] for g in groups]
            local = rows - float(window)
        looked = look_up_block(jnp.concatenate(part, 0).astype(BF16), 16, cols, local)
        turn(slice(at, at + 8), v[3] >= 0.0, v, looked)
    stores = [pltpu.make_async_copy(out, out_hbm, store_sem.at[0])]
    stores[0].start()

    for c in range(3):
        for par in range(2):
            lanes = slice(par * 128, par * 128 + 128)
            for first, n, cx, cx_step, half_y, half_step in PIECES:
                if first < BORDER:
                    piece = border_mean[c][first : first + n, lanes]
                else:
                    piece = inner_mean[c, first - BORDER : first - BORDER + n, lanes]
                start = cx * 10 + 2 * half_y + par
                means[c, pl.ds(start, n, stride=10 * cx_step + 2 * half_step), :] = piece
    load.wait()
    low_x = (shift[0] == 1).astype(jnp.int32)
    low_y = (shift[1] == 1).astype(jnp.int32)
    for c in range(3):
        for cx in range(CXL):
            flow[c, cx * 8 : cx * 8 + 8, :] = means[c, pl.ds((cx + low_x) * 10 + low_y, 8), :]
    stores.append(pltpu.make_async_copy(flow, flow_hbm, store_sem.at[1]))
    stores[1].start()
    for store in stores:
        store.wait()


def shape(*dims):
    return jax.ShapeDtypeStruct(dims, F32)


def per_device(velocity, position, leaving, grid_shift, axis_index):
    vel = velocity.reshape(3, ROWS, 128)
    pos = position.reshape(3, ROWS, 128)
    axis = axis_index.reshape(64, 128)
    leaving = leaving.reshape(4)
    vel, pos, axis, leaving, grid_shift = [
        pltpu.with_memory_space_constraint(v, pltpu.HBM) for v in (vel, pos, axis, leaving, grid_shift)
    ]
    vmem = pl.BlockSpec(memory_space=pltpu.VMEM)
    hbm = pl.BlockSpec(memory_space=pltpu.HBM)
    parts = pl.pallas_call(
        prep_kernel,
        name="prep",
        out_shape=(
            shape(8 * (BORDER + 2), 128),
            shape(2, 56, 128),
            shape(ROWS, 128),
            shape(3, 24, 256),
            shape(4, ROWS, 128),
            shape(3, ROWS, 128),
            shape(4, 80, 128),
            shape(4, 16, 128),
            shape(4, 64, 128),
            shape(4, 8, 128),
        ),
        in_specs=[hbm] * 5,
        out_specs=(vmem,) * 10,
        scratch_shapes=[
            pltpu.SMEM((4,), jnp.int32),
            pltpu.SMEM((3,), jnp.int32),
            pltpu.VMEM((3, ROWS, 128), F32),
            pltpu.VMEM((64, 128), jnp.int32),
            pltpu.VMEM((ROWS, 128), F32),
            pltpu.VMEM((ROWS, 128), F32),
            pltpu.VMEM((7 * MAIN + 16, 256), F32),
            pltpu.VMEM((2, 128, 128), F32),
            pltpu.VMEM((32, 128), F32),
            pltpu.VMEM((128, 128), F32),
            pltpu.VMEM((4, 64, 128), F32),
            pltpu.VMEM((4, 8, 128), F32),
            pltpu.SemaphoreType.DMA((5,)),
            pltpu.SemaphoreType.DMA((2, 8)),
            pltpu.SemaphoreType.DMA((2, 8)),
        ],
        compiler_params=pltpu.CompilerParams(
            collective_id=0, has_side_effects=True, vmem_limit_bytes=32 << 20
        ),
    )(leaving, grid_shift, vel, pos, axis)
    out, flow = pl.pallas_call(
        collide_kernel,
        name="collide",
        out_shape=(shape(3, SLOTS, 128), shape(3, 64, 128)),
        in_specs=[hbm] + [vmem] * 10,
        out_specs=(hbm, hbm),
        scratch_shapes=[
            pltpu.SMEM((3,), jnp.int32),
            pltpu.VMEM((3, SLOTS, 128), F32),
            pltpu.VMEM((3, 64, 128), F32),
            pltpu.VMEM((8 * BORDER, 128), F32),
            pltpu.VMEM((3, 104, 128), F32),
            pltpu.SemaphoreType.DMA,
            pltpu.SemaphoreType.DMA((2,)),
        ],
        compiler_params=pltpu.CompilerParams(vmem_limit_bytes=32 << 20),
    )(grid_shift, *parts)
    return out.reshape(3, 1, 1, SLOTS * 128), flow.reshape(3, 1, 1, 64 * 128)


def solution(mesh):
    return jax.shard_map(
        per_device,
        mesh=mesh,
        in_specs=(
            P(None, "gx", "gy", None),
            P(None, "gx", "gy", None),
            P("gx", "gy", None),
            P(),
            P("gx", "gy", None),
        ),
        out_specs=(P(None, "gx", "gy", None), P(None, "gx", "gy", None)),
        check_vma=False,
    )
```

time: 21.3 us -> 18.8 us (0.88)
  Pallas kernels: 20.5 us -> 18.1 us
    pallas_call x1, Pallas kernels: 4.29 us -> 2.33 us  [per_device(): pl.pallas_call(collide_kernel, name='collide', out_shape=(shape(3, SLOTS,...]
    pallas_call x1, Pallas kernels: 16.2 us -> 15.7 us  [per_device(): pl.pallas_call(prep_kernel, name='prep', out_shape=(shape(8 * (BORDER + 2...]
where the time goes in v4:
time: 18.8 us; the launch traced here: 18.7 us
  Pallas kernels  18.1 us (96%)
  between operations  0.64 us (3%)
    pallas_call x1, Pallas kernels, per_device(): pl.pallas_call(prep_kernel, name='prep', out_shape=(shape(8 * (BORDER + 2...  15.7 us
    pallas_call x1, Pallas kernels, per_device(): pl.pallas_call(collide_kernel, name='collide', out_shape=(shape(3, SLOTS,...  2.33 us

profile of v4, /device:TPU:1, one launch (start us, length us, event | category | flops | bytes accessed | tf_op | source)
XLA Modules:
  0.0 18.7 jit_solution(5237438122941827883)
XLA Ops:
  0.6 15.7 %prep.1 = (f32[272,128]{1,0:T(8,128)S(1)}, f32[2,56,128]{2,1,0:T(8,128)S(1)}, f32[64,128]{1,0:T(8,128)S(1)}, f32[3,24,256]{2,1,0:T(8,128)S(1)}, f32[4,64,128]{2,...) custom-call(s32[4]{0:T(128)} %bitcast.9, ...), custom_call_target="tpu_custom_call" | custom-call | tf_op jit(solution)/shard_map/prep/pallas_call | solution.py:479
  16.4 2.3 %collide.1 = (f32[3,96,128]{2,1,0:T(8,128)}, f32[3,64,128]{2,1,0:T(8,128)}) custom-call(s32[3]{0:T(128)} %shift_in.3, f32[272,128]{1,0:T(8,128)S(1)} %get-tuple-element.14.border, f32[2,56,128]{2,1,0:T(8,128)S(1)} %get-tuple-element.15.own_axis, f32[64,128]{1,0:T(8,128)S(1)} %get-tuple-element.16.ids, f32[3,24,256]{2,1,0:T(8,128)S(1)} %get-tuple-element.17.inner_mean, ...), custom_call_target="tpu_custom_call" | custom-call | tf_op jit(solution)/shard_map/collide/pallas_call | solution.py:517

commit v5 on v4

--- a/solution.py
+++ b/solution.py
@@ -107,8 +107,8 @@
 
 def prep_kernel(
     leaving_in, shift_in, vel_in, pos_in, axis_in,
-    border, own_axis, ids, inner_mean, found, vel, got_sum, got_sum_c, got_run, got_run_c,
-    leaving, shift, pos, axis, row_s, col_s, sums, run_s, prep_s, axis_s, run_o, run_oc,
+    border, own_axis, ids, inner_mean, found, vel, got_side, got_corner,
+    leaving, shift, pos, axis, row_s, col_s, sums, run_s, prep_s, axis_s, side, corner,
     load_sem, send_sem, recv_sem,
 ):
     loads = [
@@ -124,7 +124,7 @@
     for target in targets:
         pl.semaphore_signal(barrier, inc=1, device_id=target, device_id_type=MESH)
     axis_s[...] = jnp.zeros(axis_s.shape, F32)
-    run_o[...] = jnp.zeros(run_o.shape, F32)
+    side[:, 112:144, :] = jnp.zeros((4, 32, 128), F32)
     for load in loads:
         load.wait()
 
@@ -187,7 +187,14 @@
         for par in range(2):
             lanes = slice(par * 128, par * 128 + 128)
             border[pl.ds(2 * c + par, BORDER, stride=8), :] = group[:, lanes]
-    border[8 * BORDER : 8 * BORDER + 16, :] = border[0:16, :]
+    for k, start in enumerate((0, 16, 24, 8)):
+        if start == 24:
+            side[k, 0:64, :] = border[192:256, :]
+            side[k, 64:80, :] = border[0:16, :]
+        else:
+            side[k, 0:80, :] = border[8 * start : 8 * start + 80, :]
+    for k, start in enumerate((0, 8, 24, 16)):
+        corner[k, 0:16, :] = border[8 * start : 8 * start + 16, :]
 
     for cx in range(CXL):
         at = (cx + 1) * 11 + 1
@@ -198,16 +205,16 @@
             step = 11 * cx_step + 2 * half_step
             own_axis[par, first : first + n, :] = axis_s[pl.ds(start, n, stride=step), :]
         own_axis[par, 50:56, :] = jnp.zeros((6, 128), F32)
-        base = 32 + 16 * par
+        base = 112 + 16 * par
         for k, order in enumerate(
             (((8, 2), (2, 6), (0, 2)), ((24, 2), (18, 6), (16, 2)), ((0, 2), (26, 6), (24, 2)), ((16, 2), (10, 6), (8, 2)))
         ):
             at = base
             for first, n in order:
-                run_o[k, at : at + n, :] = own_axis[par, first : first + n, :]
+                side[k, at : at + n, :] = own_axis[par, first : first + n, :]
                 at += n
         for k, first in enumerate((0, 8, 24, 16)):
-            run_oc[k, 4 + 2 * par : 6 + 2 * par, :] = own_axis[par, first : first + 2, :]
+            corner[k, 20 + 2 * par : 22 + 2 * par, :] = own_axis[par, first : first + 2, :]
 
     slot = iota((8, 128), 0) * 128 + iota((8, 128), 1)
     lane = iota((8, 128), 1)
@@ -255,8 +262,8 @@
             run_s[d, 64:72, :] = jnp.ones((8, 128), F32)
             run_s[d, 72:128, :] = jnp.zeros((56, 128), F32)
         for c in range(3):
-            run_o[d, 8 * c : 8 * c + 8, :] = values[c]
-        run_o[d, 24:32, :] = jnp.where(kept, moved(d, run_row) * 256.0 + run_col, -1.0)
+            side[d, 80 + 8 * c : 88 + 8 * c, :] = values[c]
+        side[d, 104:112, :] = jnp.where(kept, moved(d, run_row) * 256.0 + run_col, -1.0)
 
     flag = jnp.concatenate([f.astype(F32) for f in flags], 0)
     flag16 = flag.astype(BF16)
@@ -276,37 +283,24 @@
             packed = dot_nt(rows, jnp.concatenate(hits, 1))
             k = d * 2 + s
             for c in range(3):
-                run_oc[k, c : c + 1, :] = packed[2 * c : 2 * c + 1] + packed[2 * c + 1 : 2 * c + 2]
+                corner[k, 16 + c : 17 + c, :] = packed[2 * c : 2 * c + 1] + packed[2 * c + 1 : 2 * c + 2]
             there = (packed[6:7] + (16.0 - 32.0 * d)) * 256.0 + packed[7:8]
-            run_oc[k, 3:4, :] = jnp.where(packed[8:9] > 0.5, there, -1.0)
+            corner[k, 19:20, :] = jnp.where(packed[8:9] > 0.5, there, -1.0)
 
     pl.semaphore_wait(barrier, 8)
     copies = []
     for k in (4, 5, 6, 7, 0, 1, 2, 3):
-        if k < 4:
-            source = border.at[pl.ds(8 * (0, 16, 24, 8)[k], 80), :]
-            target = got_sum.at[k]
-        else:
-            source = border.at[pl.ds(8 * (0, 8, 24, 16)[k - 4], 16), :]
-            target = got_sum_c.at[k - 4]
-        copies.append((0, k, source, target))
-    for k in (4, 5, 6, 7, 0, 1, 2, 3):
-        if k < 4:
-            copies.append((1, k, run_o.at[k], got_run.at[k]))
-        else:
-            copies.append((1, k, run_oc.at[k - 4], got_run_c.at[k - 4]))
-    sent = []
-    for kind, k, source, target in copies:
+        source, target = (side.at[k], got_side.at[k]) if k < 4 else (corner.at[k - 4], got_corner.at[k - 4])
         copy = pltpu.make_async_remote_copy(
             src_ref=source,
             dst_ref=target,
-            send_sem=send_sem.at[kind, k],
-            recv_sem=recv_sem.at[kind, k],
+            send_sem=send_sem.at[k],
+            recv_sem=recv_sem.at[k],
             device_id=targets[k],
             device_id_type=MESH,
         )
         copy.start()
-        sent.append(copy)
+        copies.append(copy)
 
     def inner(group):
         at = group * MAIN + BORDER
@@ -331,18 +325,18 @@
     gone = starts[3] + counts[3]
     place = iota((ROWS, 128), 0) * 128 + iota((ROWS, 128), 1)
     ids[...] = jnp.where(place >= gone, ids[...], -1.0)
-    for copy in sent:
+    for copy in copies:
         copy.wait()
 
 
 def collide_kernel(
-    shift_in, border, own_axis, ids, inner_mean, found, vel, got_sum, got_sum_c, got_run, got_run_c,
+    shift_in, border, own_axis, ids, inner_mean, found, vel, got_side, got_corner,
     out_hbm, flow_hbm,
     shift, out, flow, total, means, load_sem, store_sem,
 ):
     load = pltpu.make_async_copy(shift_in, shift, load_sem)
     load.start()
-    total[...] = border[0 : 8 * BORDER, :]
+    total[...] = border[...]
     for k, places in enumerate(
         (
             ((24, 0, 2), (18, 2, 6), (16, 8, 2)),
@@ -352,22 +346,22 @@
         )
     ):
         for mine, theirs, n in places:
-            total[8 * mine : 8 * (mine + n), :] += got_sum[k, 8 * theirs : 8 * (theirs + n), :]
+            total[8 * mine : 8 * (mine + n), :] += got_side[k, 8 * theirs : 8 * (theirs + n), :]
     for k, mine in enumerate((16, 24, 8, 0)):
-        total[8 * mine : 8 * mine + 16, :] += got_sum_c[k]
+        total[8 * mine : 8 * mine + 16, :] += got_corner[k, 0:16, :]
     numbers = []
     for par in range(2):
         number = own_axis[par, 0:BORDER, :]
-        at = 32 + 16 * par
+        at = 112 + 16 * par
         zero = jnp.zeros((16, 128), F32)
         for k, (before, after) in enumerate(((16, 0), (0, 16), (8, 8))):
-            strip = got_run[k, at : at + 16, :]
+            strip = got_side[k, at : at + 16, :]
             parts = [jnp.zeros((before, 128), F32)] * (before > 0) + [strip]
             parts += [jnp.zeros((after, 128), F32)] * (after > 0)
             number = number + jnp.concatenate(parts, 0)
-        strip = got_run[3, at : at + 16, :]
+        strip = got_side[3, at : at + 16, :]
         number = number + jnp.concatenate([strip[8:16], zero, strip[0:8]], 0)
-        pair = [got_run_c[k, 4 + 2 * par : 6 + 2 * par, :] for k in range(4)]
+        pair = [got_corner[k, 20 + 2 * par : 22 + 2 * par, :] for k in range(4)]
         gap = jnp.zeros((6, 128), F32)
         number = number + jnp.concatenate([pair[3], gap, pair[2], gap, pair[0], gap, pair[1], gap], 0)
         numbers.append(number)
@@ -405,6 +399,24 @@
             turned = mean[c] + COS_TURN * w[c] + SIN_TURN * cross[c] + along * a[c]
             out[c, at, :] = jnp.where(live, turned, 0.0)
 
+    slot = iota((8, 128), 0) * 128 + iota((8, 128), 1)
+    arrived = []
+    for k in (1, 0, 3, 2):
+        v = [got_side[k, 80 + 8 * c : 88 + 8 * c, :] for c in range(4)]
+        if k > 1:
+            first, second = ((2, 0), (3, 1))[k - 2]
+            n0 = jnp.sum((v[3] >= 0.0).astype(jnp.int32))
+            n1 = jnp.sum((got_corner[first, 19:20, :] >= 0.0).astype(jnp.int32))
+            in_first = (slot >= n0) & (slot < n0 + n1)
+            in_second = (slot >= n0 + n1) & (slot < n0 + n1 + 128)
+            by1, by2 = lax.rem(n0, 128), lax.rem(n0 + n1, 128)
+            for c in range(4):
+                at = slice(16 + c, 17 + c)
+                one = pltpu.roll(jnp.broadcast_to(got_corner[first, at, :], (8, 128)), by1, 1)
+                two = pltpu.roll(jnp.broadcast_to(got_corner[second, at, :], (8, 128)), by2, 1)
+                v[c] = jnp.where(in_first, one, jnp.where(in_second, two, v[c]))
+        arrived.append(v)
+
     out[:, 0:8, :] = jnp.zeros((3, 8, 128), F32)
     for b in range(1, 8):
         at = slice(8 * b, 8 * b + 8)
@@ -412,21 +424,14 @@
         rows = jnp.floor(block * (1.0 / 256.0))
         looked = look_up_block(table, BORDER, block - rows * 256.0, rows)
         turn(at, block >= 0.0, [vel[c, at, :] for c in range(3)], [looked[c] + found[c, at, :] for c in range(4)])
-
-    slot = iota((8, 128), 0) * 128 + iota((8, 128), 1)
-    for at, k, window in ((64, 1, 0), (72, 0, 16), (80, 3, 24), (88, 2, 8)):
-        v = [got_run[k, 8 * c : 8 * c + 8, :] for c in range(4)]
-        if k > 1:
-            first, second = ((2, 0), (3, 1))[k - 2]
-            n0 = jnp.sum((v[3] >= 0.0).astype(jnp.int32))
-            n1 = jnp.sum((got_run_c[first, 3:4, :] >= 0.0).astype(jnp.int32))
-            in_first = (slot >= n0) & (slot < n0 + n1)
-            in_second = (slot >= n0 + n1) & (slot < n0 + n1 + 128)
-            by1, by2 = lax.rem(n0, 128), lax.rem(n0 + n1, 128)
-            for c in range(4):
-                one = pltpu.roll(jnp.broadcast_to(got_run_c[first, c : c + 1, :], (8, 128)), by1, 1)
-                two = pltpu.roll(jnp.broadcast_to(got_run_c[second, c : c + 1, :], (8, 128)), by2, 1)
-                v[c] = jnp.where(in_first, one, jnp.where(in_second, two, v[c]))
+    stores = []
+
+    def store(source, target):
+        copy = pltpu.make_async_copy(source, target, store_sem.at[len(stores)])
+        copy.start()
+        stores.append(copy)
+
+    for v, at, window in zip(arrived, (64, 72, 80, 88), (0, 16, 24, 8)):
         rows = jnp.floor(v[3] * (1.0 / 256.0))
         cols = v[3] - rows * 256.0
         if window == 24:
@@ -437,8 +442,7 @@
             local = rows - float(window)
         looked = look_up_block(jnp.concatenate(part, 0).astype(BF16), 16, cols, local)
         turn(slice(at, at + 8), v[3] >= 0.0, v, looked)
-    stores = [pltpu.make_async_copy(out, out_hbm, store_sem.at[0])]
-    stores[0].start()
+    store(out, out_hbm)
 
     for c in range(3):
         for par in range(2):
@@ -456,10 +460,9 @@
     for c in range(3):
         for cx in range(CXL):
             flow[c, cx * 8 : cx * 8 + 8, :] = means[c, pl.ds((cx + low_x) * 10 + low_y, 8), :]
-    stores.append(pltpu.make_async_copy(flow, flow_hbm, store_sem.at[1]))
-    stores[1].start()
-    for store in stores:
-        store.wait()
+    store(flow, flow_hbm)
+    for copy in stores:
+        copy.wait()
 
 
 def shape(*dims):
@@ -480,19 +483,17 @@
         prep_kernel,
         name="prep",
         out_shape=(
-            shape(8 * (BORDER + 2), 128),
+            shape(8 * BORDER, 128),
             shape(2, 56, 128),
             shape(ROWS, 128),
             shape(3, 24, 256),
             shape(4, ROWS, 128),
             shape(3, ROWS, 128),
-            shape(4, 80, 128),
-            shape(4, 16, 128),
-            shape(4, 64, 128),
-            shape(4, 8, 128),
+            shape(4, 144, 128),
+            shape(4, 24, 128),
         ),
         in_specs=[hbm] * 5,
-        out_specs=(vmem,) * 10,
+        out_specs=(vmem,) * 8,
         scratch_shapes=[
             pltpu.SMEM((4,), jnp.int32),
             pltpu.SMEM((3,), jnp.int32),
@@ -504,11 +505,11 @@
             pltpu.VMEM((2, 128, 128), F32),
             pltpu.VMEM((32, 128), F32),
             pltpu.VMEM((128, 128), F32),
-            pltpu.VMEM((4, 64, 128), F32),
-            pltpu.VMEM((4, 8, 128), F32),
+            pltpu.VMEM((4, 144, 128), F32),
+            pltpu.VMEM((4, 24, 128), F32),
             pltpu.SemaphoreType.DMA((5,)),
-            pltpu.SemaphoreType.DMA((2, 8)),
-            pltpu.SemaphoreType.DMA((2, 8)),
+            pltpu.SemaphoreType.DMA((8,)),
+            pltpu.SemaphoreType.DMA((8,)),
         ],
         compiler_params=pltpu.CompilerParams(
             collective_id=0, has_side_effects=True, vmem_limit_bytes=32 << 20
@@ -518,7 +519,7 @@
         collide_kernel,
         name="collide",
         out_shape=(shape(3, SLOTS, 128), shape(3, 64, 128)),
-        in_specs=[hbm] + [vmem] * 10,
+        in_specs=[hbm] + [vmem] * 8,
         out_specs=(hbm, hbm),
         scratch_shapes=[
             pltpu.SMEM((3,), jnp.int32),
@@ -527,7 +528,7 @@
             pltpu.VMEM((8 * BORDER, 128), F32),
             pltpu.VMEM((3, 104, 128), F32),
             pltpu.SemaphoreType.DMA,
-            pltpu.SemaphoreType.DMA((2,)),
+            pltpu.SemaphoreType.DMA((3,)),
         ],
         compiler_params=pltpu.CompilerParams(vmem_limit_bytes=32 << 20),
     )(grid_shift, *parts)

time: 18.8 us -> 17.8 us (0.947)
  Pallas kernels: 18.1 us -> 17 us
    pallas_call x1, Pallas kernels: 15.7 us -> 14.7 us  [per_device(): pl.pallas_call(prep_kernel, name='prep', out_shape=(shape(8 * BORDER, 128...]
where the time goes in v5:
time: 17.8 us; the launch traced here: 17.7 us
  Pallas kernels  17 us (96%)
  between operations  0.64 us (4%)
    pallas_call x1, Pallas kernels, per_device(): pl.pallas_call(prep_kernel, name='prep', out_shape=(shape(8 * BORDER, 128...  14.7 us
    pallas_call x1, Pallas kernels, per_device(): pl.pallas_call(collide_kernel, name='collide', out_shape=(shape(3, SLOTS,...  2.33 us

profile of v5, /device:TPU:1, one launch (start us, length us, event | category | flops | bytes accessed | tf_op | source)
XLA Modules:
  0.0 17.7 jit_solution(4287164577645492971)
XLA Ops:
  0.6 14.7 %prep.1 = (f32[256,128]{1,0:T(8,128)S(1)}, f32[2,56,128]{2,1,0:T(8,128)S(1)}, f32[64,128]{1,0:T(8,128)S(1)}, f32[3,24,256]{2,1,0:T(8,128)S(1)}, f32[4,64,128]{2,...) custom-call(s32[4]{0:T(128)} %bitcast.9, s32[3]{0:T(128)} %shift_in.3, ...), custom_call_target="tpu_custom_call" | custom-call | tf_op jit(solution)/shard_map/prep/pallas_call | solution.py:482
  15.3 2.3 %collide.1 = (f32[3,96,128]{2,1,0:T(8,128)}, f32[3,64,128]{2,1,0:T(8,128)}) custom-call(s32[3]{0:T(128)} %shift_in.3, f32[256,128]{1,0:T(8,128)S(1)} %get-tuple-element.12.border, f32[2,56,128]{2,1,0:T(8,128)S(1)} %get-tuple-element.13.own_axis, f32[64,128]{1,0:T(8,128)S(1)} %get-tuple-element.14.ids, f32[3,24,256]{2,1,0:T(8,128)S(1)} %get-tuple-element.15.inner_mean, ...), custom_call_target="tpu_custom_call" | custom-call | tf_op jit(solution)/shard_map/collide/pallas_call | solution.py:518

commit v6 on v5

--- a/solution.py
+++ b/solution.py
@@ -111,6 +111,10 @@
     leaving, shift, pos, axis, row_s, col_s, sums, run_s, prep_s, axis_s, side, corner,
     load_sem, send_sem, recv_sem,
 ):
+    targets = neighbours()
+    barrier = pltpu.get_barrier_semaphore()
+    for target in targets:
+        pl.semaphore_signal(barrier, inc=1, device_id=target, device_id_type=MESH)
     loads = [
         pltpu.make_async_copy(source, target, load_sem.at[k])
         for k, (source, target) in enumerate(
@@ -119,12 +123,10 @@
     ]
     for load in loads:
         load.start()
-    targets = neighbours()
-    barrier = pltpu.get_barrier_semaphore()
-    for target in targets:
-        pl.semaphore_signal(barrier, inc=1, device_id=target, device_id_type=MESH)
     axis_s[...] = jnp.zeros(axis_s.shape, F32)
-    side[:, 112:144, :] = jnp.zeros((4, 32, 128), F32)
+    for k in (0, 2):
+        side[k, 112:144, :] = jnp.zeros((32, 128), F32)
+    corner[:, 20:24, :] = jnp.zeros((4, 4, 128), F32)
     for load in loads:
         load.wait()
 
@@ -206,15 +208,12 @@
             own_axis[par, first : first + n, :] = axis_s[pl.ds(start, n, stride=step), :]
         own_axis[par, 50:56, :] = jnp.zeros((6, 128), F32)
         base = 112 + 16 * par
-        for k, order in enumerate(
-            (((8, 2), (2, 6), (0, 2)), ((24, 2), (18, 6), (16, 2)), ((0, 2), (26, 6), (24, 2)), ((16, 2), (10, 6), (8, 2)))
-        ):
+        for k, order in ((0, ((8, 2), (2, 6), (0, 2))), (2, ((0, 2), (26, 6), (24, 2)))):
             at = base
             for first, n in order:
                 side[k, at : at + n, :] = own_axis[par, first : first + n, :]
                 at += n
-        for k, first in enumerate((0, 8, 24, 16)):
-            corner[k, 20 + 2 * par : 22 + 2 * par, :] = own_axis[par, first : first + 2, :]
+        corner[0, 20 + 2 * par : 22 + 2 * par, :] = own_axis[par, 0:2, :]
 
     slot = iota((8, 128), 0) * 128 + iota((8, 128), 1)
     lane = iota((8, 128), 1)
@@ -289,18 +288,33 @@
 
     pl.semaphore_wait(barrier, 8)
     copies = []
-    for k in (4, 5, 6, 7, 0, 1, 2, 3):
-        source, target = (side.at[k], got_side.at[k]) if k < 4 else (corner.at[k - 4], got_corner.at[k - 4])
-        copy = pltpu.make_async_remote_copy(
-            src_ref=source,
-            dst_ref=target,
-            send_sem=send_sem.at[k],
-            recv_sem=recv_sem.at[k],
-            device_id=targets[k],
-            device_id_type=MESH,
+    for k in range(8):
+        if k < 4:
+            size = 144 if k in (0, 2) else 112
+            source, target = side.at[k, pl.ds(0, size), :], got_side.at[k, pl.ds(0, size), :]
+        else:
+            source, target = corner.at[k - 4], got_corner.at[k - 4]
+        copies.append(
+            pltpu.make_async_remote_copy(
+                src_ref=source,
+                dst_ref=target,
+                send_sem=send_sem.at[k],
+                recv_sem=recv_sem.at[k],
+                device_id=targets[k],
+                device_id_type=MESH,
+            )
         )
-        copy.start()
-        copies.append(copy)
+    right_first = lax.rem(lax.axis_index("gx"), 4) == 3
+
+    @pl.when(right_first)
+    def _():
+        for k in (6, 7, 1, 4, 5, 0, 2, 3):
+            copies[k].start()
+
+    @pl.when(jnp.logical_not(right_first))
+    def _():
+        for k in (4, 5, 0, 6, 7, 1, 2, 3):
+            copies[k].start()
 
     def inner(group):
         at = group * MAIN + BORDER
@@ -353,17 +367,11 @@
     for par in range(2):
         number = own_axis[par, 0:BORDER, :]
         at = 112 + 16 * par
-        zero = jnp.zeros((16, 128), F32)
-        for k, (before, after) in enumerate(((16, 0), (0, 16), (8, 8))):
-            strip = got_side[k, at : at + 16, :]
-            parts = [jnp.zeros((before, 128), F32)] * (before > 0) + [strip]
-            parts += [jnp.zeros((after, 128), F32)] * (after > 0)
-            number = number + jnp.concatenate(parts, 0)
-        strip = got_side[3, at : at + 16, :]
-        number = number + jnp.concatenate([strip[8:16], zero, strip[0:8]], 0)
-        pair = [got_corner[k, 20 + 2 * par : 22 + 2 * par, :] for k in range(4)]
-        gap = jnp.zeros((6, 128), F32)
-        number = number + jnp.concatenate([pair[3], gap, pair[2], gap, pair[0], gap, pair[1], gap], 0)
+        gap = jnp.zeros((16, 128), F32)
+        number = number + jnp.concatenate([gap, got_side[0, at : at + 16, :]], 0)
+        number = number + jnp.concatenate([gap[0:8], got_side[2, at : at + 16, :], gap[0:8]], 0)
+        pair = got_corner[0, 20 + 2 * par : 22 + 2 * par, :]
+        number = number + jnp.concatenate([gap, pair, gap[0:14]], 0)
         numbers.append(number)
     groups = [None] * 7
     most = [jnp.maximum(total[pl.ds(par, BORDER, stride=8), :], 1.0) for par in range(2)]
@@ -417,13 +425,6 @@
                 v[c] = jnp.where(in_first, one, jnp.where(in_second, two, v[c]))
         arrived.append(v)
 
-    out[:, 0:8, :] = jnp.zeros((3, 8, 128), F32)
-    for b in range(1, 8):
-        at = slice(8 * b, 8 * b + 8)
-        block = ids[at, :]
-        rows = jnp.floor(block * (1.0 / 256.0))
-        looked = look_up_block(table, BORDER, block - rows * 256.0, rows)
-        turn(at, block >= 0.0, [vel[c, at, :] for c in range(3)], [looked[c] + found[c, at, :] for c in range(4)])
     stores = []
 
     def store(source, target):
@@ -442,6 +443,14 @@
             local = rows - float(window)
         looked = look_up_block(jnp.concatenate(part, 0).astype(BF16), 16, cols, local)
         turn(slice(at, at + 8), v[3] >= 0.0, v, looked)
+
+    out[:, 0:8, :] = jnp.zeros((3, 8, 128), F32)
+    for b in range(1, 8):
+        at = slice(8 * b, 8 * b + 8)
+        block = ids[at, :]
+        rows = jnp.floor(block * (1.0 / 256.0))
+        looked = look_up_block(table, BORDER, block - rows * 256.0, rows)
+        turn(at, block >= 0.0, [vel[c, at, :] for c in range(3)], [looked[c] + found[c, at, :] for c in range(4)])
     store(out, out_hbm)
 
     for c in range(3):

time: 17.8 us -> 17.8 us (level)
  no operation moved by 1% of the time
where the time goes in v6:
time: 17.8 us; the launch traced here: 17.7 us
  Pallas kernels  17 us (96%)
  between operations  0.64 us (4%)
    pallas_call x1, Pallas kernels, per_device(): pl.pallas_call(prep_kernel, name='prep', out_shape=(shape(8 * BORDER, 128...  14.7 us
    pallas_call x1, Pallas kernels, per_device(): pl.pallas_call(collide_kernel, name='collide', out_shape=(shape(3, SLOTS,...  2.34 us

profile of v6, /device:TPU:1, one launch (start us, length us, event | category | flops | bytes accessed | tf_op | source)
XLA Modules:
  0.0 17.7 jit_solution(7134408582534184730)
XLA Ops:
  0.6 14.7 %prep.1 = (f32[256,128]{1,0:T(8,128)S(1)}, f32[2,56,128]{2,1,0:T(8,128)S(1)}, f32[64,128]{1,0:T(8,128)S(1)}, f32[3,24,256]{2,1,0:T(8,128)S(1)}, f32[4,64,128]{2,...) custom-call(s32[4]{0:T(128)} %bitcast.9, s32[3]{0:T(128)} %shift_in.3, ...), custom_call_target="tpu_custom_call" | custom-call | tf_op jit(solution)/shard_map/prep/pallas_call | solution.py:491
  15.3 2.3 %collide.1 = (f32[3,96,128]{2,1,0:T(8,128)}, f32[3,64,128]{2,1,0:T(8,128)}) custom-call(s32[3]{0:T(128)} %shift_in.3, f32[256,128]{1,0:T(8,128)S(1)} %get-tuple-element.12.border, f32[2,56,128]{2,1,0:T(8,128)S(1)} %get-tuple-element.13.own_axis, f32[64,128]{1,0:T(8,128)S(1)} %get-tuple-element.14.ids, f32[3,24,256]{2,1,0:T(8,128)S(1)} %get-tuple-element.15.inner_mean, ...), custom_call_target="tpu_custom_call" | custom-call | tf_op jit(solution)/shard_map/collide/pallas_call | solution.py:527

commit v7 on v6

--- a/solution.py
+++ b/solution.py
@@ -113,8 +113,15 @@
 ):
     targets = neighbours()
     barrier = pltpu.get_barrier_semaphore()
-    for target in targets:
-        pl.semaphore_signal(barrier, inc=1, device_id=target, device_id_type=MESH)
+    is_first = lax.rem(lax.axis_index("gy"), 16) == 0
+    is_last = lax.rem(lax.axis_index("gy"), 16) == 15
+
+    def greet(places):
+        for k in places:
+            pl.semaphore_signal(barrier, inc=1, device_id=targets[k], device_id_type=MESH)
+
+    greet((4, 6, 0, 1, 2))
+    pl.when(jnp.logical_not(is_last))(lambda: greet((5, 7, 3)))
     loads = [
         pltpu.make_async_copy(source, target, load_sem.at[k])
         for k, (source, target) in enumerate(
@@ -286,7 +293,7 @@
             there = (packed[6:7] + (16.0 - 32.0 * d)) * 256.0 + packed[7:8]
             corner[k, 19:20, :] = jnp.where(packed[8:9] > 0.5, there, -1.0)
 
-    pl.semaphore_wait(barrier, 8)
+    pl.semaphore_wait(barrier, jnp.where(is_first, 5, 8))
     copies = []
     for k in range(8):
         if k < 4:
@@ -304,16 +311,12 @@
                 device_id_type=MESH,
             )
         )
-    right_first = lax.rem(lax.axis_index("gx"), 4) == 3
-
-    @pl.when(right_first)
+    for k in (5, 7, 0, 1, 3):
+        copies[k].start()
+
+    @pl.when(jnp.logical_not(is_first))
     def _():
-        for k in (6, 7, 1, 4, 5, 0, 2, 3):
-            copies[k].start()
-
-    @pl.when(jnp.logical_not(right_first))
-    def _():
-        for k in (4, 5, 0, 6, 7, 1, 2, 3):
+        for k in (4, 6, 2):
             copies[k].start()
 
     def inner(group):
@@ -339,8 +342,14 @@
     gone = starts[3] + counts[3]
     place = iota((ROWS, 128), 0) * 128 + iota((ROWS, 128), 1)
     ids[...] = jnp.where(place >= gone, ids[...], -1.0)
+
+    for there, back in ((7, 4), (5, 6), (3, 2)):
+        copies[there].wait_recv()
+        pl.when(is_first)(copies[back].start)
+    for k in (0, 1, 2, 4, 6):
+        copies[k].wait_recv()
     for copy in copies:
-        copy.wait()
+        copy.wait_send()
 
 
 def collide_kernel(

time: 17.8 us -> 19.4 us (1.090)
  the two profiles are of different devices: /device:TPU:1 before, /device:TPU:8 now
where the time goes in v7:
time: 19.4 us; the launch traced here: 19.2 us
  Pallas kernels  18.6 us (96%)
  between operations  0.64 us (3%)
    pallas_call x1, Pallas kernels, per_device(): pl.pallas_call(prep_kernel, name='prep', out_shape=(shape(8 * BORDER, 128...  16.3 us
    pallas_call x1, Pallas kernels, per_device(): pl.pallas_call(collide_kernel, name='collide', out_shape=(shape(3, SLOTS,...  2.33 us

profile of v7, /device:TPU:8, one launch (start us, length us, event | category | flops | bytes accessed | tf_op | source)
XLA Modules:
  0.0 19.2 jit_solution(2476479782142501115)
XLA Ops:
  0.6 16.3 %prep.1 = (f32[256,128]{1,0:T(8,128)S(1)}, f32[2,56,128]{2,1,0:T(8,128)S(1)}, f32[64,128]{1,0:T(8,128)S(1)}, f32[3,24,256]{2,1,0:T(8,128)S(1)}, f32[4,64,128]{2,...) custom-call(s32[4]{0:T(128)} %bitcast.9, s32[3]{0:T(128)} %shift_in.3, ...), custom_call_target="tpu_custom_call" | custom-call | tf_op jit(solution)/shard_map/prep/pallas_call | solution.py:500
  16.9 2.3 %collide.1 = (f32[3,96,128]{2,1,0:T(8,128)}, f32[3,64,128]{2,1,0:T(8,128)}) custom-call(s32[3]{0:T(128)} %shift_in.3, f32[256,128]{1,0:T(8,128)S(1)} %get-tuple-element.12.border, f32[2,56,128]{2,1,0:T(8,128)S(1)} %get-tuple-element.13.own_axis, f32[64,128]{1,0:T(8,128)S(1)} %get-tuple-element.14.ids, f32[3,24,256]{2,1,0:T(8,128)S(1)} %get-tuple-element.15.inner_mean, ...), custom_call_target="tpu_custom_call" | custom-call | tf_op jit(solution)/shard_map/collide/pallas_call | solution.py:536

commit v8 on v6

--- a/solution.py
+++ b/solution.py
@@ -113,8 +113,8 @@
 ):
     targets = neighbours()
     barrier = pltpu.get_barrier_semaphore()
-    for target in targets:
-        pl.semaphore_signal(barrier, inc=1, device_id=target, device_id_type=MESH)
+    for k in (7, 5, 6, 4, 1, 0, 3, 2):
+        pl.semaphore_signal(barrier, inc=1, device_id=targets[k], device_id_type=MESH)
     loads = [
         pltpu.make_async_copy(source, target, load_sem.at[k])
         for k, (source, target) in enumerate(
@@ -304,17 +304,8 @@
                 device_id_type=MESH,
             )
         )
-    right_first = lax.rem(lax.axis_index("gx"), 4) == 3
-
-    @pl.when(right_first)
-    def _():
-        for k in (6, 7, 1, 4, 5, 0, 2, 3):
-            copies[k].start()
-
-    @pl.when(jnp.logical_not(right_first))
-    def _():
-        for k in (4, 5, 0, 6, 7, 1, 2, 3):
-            copies[k].start()
+    for k in (7, 5, 6, 4, 1, 0, 3, 2):
+        copies[k].start()
 
     def inner(group):
         at = group * MAIN + BORDER
@@ -432,6 +423,14 @@
         copy.start()
         stores.append(copy)
 
+    out[:, 0:8, :] = jnp.zeros((3, 8, 128), F32)
+    for b in range(1, 8):
+        at = slice(8 * b, 8 * b + 8)
+        block = ids[at, :]
+        rows = jnp.floor(block * (1.0 / 256.0))
+        looked = look_up_block(table, BORDER, block - rows * 256.0, rows)
+        turn(at, block >= 0.0, [vel[c, at, :] for c in range(3)], [looked[c] + found[c, at, :] for c in range(4)])
+
     for v, at, window in zip(arrived, (64, 72, 80, 88), (0, 16, 24, 8)):
         rows = jnp.floor(v[3] * (1.0 / 256.0))
         cols = v[3] - rows * 256.0
@@ -443,14 +442,6 @@
             local = rows - float(window)
         looked = look_up_block(jnp.concatenate(part, 0).astype(BF16), 16, cols, local)
         turn(slice(at, at + 8), v[3] >= 0.0, v, looked)
-
-    out[:, 0:8, :] = jnp.zeros((3, 8, 128), F32)
-    for b in range(1, 8):
-        at = slice(8 * b, 8 * b + 8)
-        block = ids[at, :]
-        rows = jnp.floor(block * (1.0 / 256.0))
-        looked = look_up_block(table, BORDER, block - rows * 256.0, rows)
-        turn(at, block >= 0.0, [vel[c, at, :] for c in range(3)], [looked[c] + found[c, at, :] for c in range(4)])
     store(out, out_hbm)
 
     for c in range(3):

time: 17.8 us -> 17.7 us (level)
  no operation moved by 1% of the time
where the time goes in v8:
time: 17.7 us; the launch traced here: 17.6 us
  Pallas kernels  17 us (96%)
  between operations  0.64 us (4%)
    pallas_call x1, Pallas kernels, per_device(): pl.pallas_call(prep_kernel, name='prep', out_shape=(shape(8 * BORDER, 128...  14.6 us
    pallas_call x1, Pallas kernels, per_device(): pl.pallas_call(collide_kernel, name='collide', out_shape=(shape(3, SLOTS,...  2.35 us

profile of v8, /device:TPU:1, one launch (start us, length us, event | category | flops | bytes accessed | tf_op | source)
XLA Modules:
  0.0 17.6 jit_solution(12387044231081956496)
XLA Ops:
  0.6 14.6 %prep.1 = (f32[256,128]{1,0:T(8,128)S(1)}, f32[2,56,128]{2,1,0:T(8,128)S(1)}, f32[64,128]{1,0:T(8,128)S(1)}, f32[3,24,256]{2,1,0:T(8,128)S(1)}, f32[4,64,128]{2,...) custom-call(s32[4]{0:T(128)} %bitcast.9, s32[3]{0:T(128)} %shift_in.3, ...), custom_call_target="tpu_custom_call" | custom-call | tf_op jit(solution)/shard_map/prep/pallas_call | solution.py:482
  15.3 2.3 %collide.1 = (f32[3,96,128]{2,1,0:T(8,128)}, f32[3,64,128]{2,1,0:T(8,128)}) custom-call(s32[3]{0:T(128)} %shift_in.3, f32[256,128]{1,0:T(8,128)S(1)} %get-tuple-element.12.border, f32[2,56,128]{2,1,0:T(8,128)S(1)} %get-tuple-element.13.own_axis, f32[64,128]{1,0:T(8,128)S(1)} %get-tuple-element.14.ids, f32[3,24,256]{2,1,0:T(8,128)S(1)} %get-tuple-element.15.inner_mean, ...), custom_call_target="tpu_custom_call" | custom-call | tf_op jit(solution)/shard_map/collide/pallas_call | solution.py:518

commit v9 on v6

--- a/solution.py
+++ b/solution.py
@@ -304,17 +304,8 @@
                 device_id_type=MESH,
             )
         )
-    right_first = lax.rem(lax.axis_index("gx"), 4) == 3
-
-    @pl.when(right_first)
-    def _():
-        for k in (6, 7, 1, 4, 5, 0, 2, 3):
-            copies[k].start()
-
-    @pl.when(jnp.logical_not(right_first))
-    def _():
-        for k in (4, 5, 0, 6, 7, 1, 2, 3):
-            copies[k].start()
+    for k in (4, 5, 6, 7, 0, 1, 2, 3):
+        copies[k].start()
 
     def inner(group):
         at = group * MAIN + BORDER
@@ -350,19 +341,23 @@
 ):
     load = pltpu.make_async_copy(shift_in, shift, load_sem)
     load.start()
-    total[...] = border[...]
-    for k, places in enumerate(
-        (
-            ((24, 0, 2), (18, 2, 6), (16, 8, 2)),
-            ((8, 0, 2), (2, 2, 6), (0, 8, 2)),
-            ((16, 0, 2), (10, 2, 6), (8, 8, 2)),
-            ((0, 0, 2), (26, 2, 6), (24, 8, 2)),
-        )
+    for first, n, parts in (
+        (0, 2, ((1, 8), (3, 0), (None, 3))),
+        (2, 6, ((1, 2),)),
+        (8, 2, ((1, 0), (2, 8), (None, 2))),
+        (10, 6, ((2, 2),)),
+        (16, 2, ((0, 8), (2, 0), (None, 0))),
+        (18, 6, ((0, 2),)),
+        (24, 2, ((0, 0), (3, 8), (None, 1))),
+        (26, 6, ((3, 2),)),
     ):
-        for mine, theirs, n in places:
-            total[8 * mine : 8 * (mine + n), :] += got_side[k, 8 * theirs : 8 * (theirs + n), :]
-    for k, mine in enumerate((16, 24, 8, 0)):
-        total[8 * mine : 8 * mine + 16, :] += got_corner[k, 0:16, :]
+        value = border[8 * first : 8 * (first + n), :]
+        for k, at in parts:
+            if k is None:
+                value = value + got_corner[at, 0:16, :]
+            else:
+                value = value + got_side[k, 8 * at : 8 * (at + n), :]
+        total[8 * first : 8 * (first + n), :] = value
     numbers = []
     for par in range(2):
         number = own_axis[par, 0:BORDER, :]
@@ -492,7 +487,7 @@
         prep_kernel,
         name="prep",
         out_shape=(
-            shape(8 * BORDER, 128),
+            shape(8 * BORDER + 8, 128),
             shape(2, 56, 128),
             shape(ROWS, 128),
             shape(3, 24, 256),
@@ -511,9 +506,9 @@
             pltpu.VMEM((ROWS, 128), F32),
             pltpu.VMEM((ROWS, 128), F32),
             pltpu.VMEM((7 * MAIN + 16, 256), F32),
-            pltpu.VMEM((2, 128, 128), F32),
+            pltpu.VMEM((2, 136, 128), F32),
             pltpu.VMEM((32, 128), F32),
-            pltpu.VMEM((128, 128), F32),
+            pltpu.VMEM((144, 128), F32),
             pltpu.VMEM((4, 144, 128), F32),
             pltpu.VMEM((4, 24, 128), F32),
             pltpu.SemaphoreType.DMA((5,)),
@@ -534,8 +529,8 @@
             pltpu.SMEM((3,), jnp.int32),
             pltpu.VMEM((3, SLOTS, 128), F32),
             pltpu.VMEM((3, 64, 128), F32),
-            pltpu.VMEM((8 * BORDER, 128), F32),
-            pltpu.VMEM((3, 104, 128), F32),
+            pltpu.VMEM((8 * BORDER + 8, 128), F32),
+            pltpu.VMEM((3, 112, 128), F32),
             pltpu.SemaphoreType.DMA,
             pltpu.SemaphoreType.DMA((3,)),
         ],

time: 17.8 us -> 17.8 us (level)
  no operation moved by 1% of the time
where the time goes in v9:
time: 17.8 us; the launch traced here: 17.7 us
  Pallas kernels  17 us (96%)
  between operations  0.64 us (4%)
    pallas_call x1, Pallas kernels, per_device(): pl.pallas_call(prep_kernel, name='prep', out_shape=(shape(8 * BORDER + 8,...  14.7 us
    pallas_call x1, Pallas kernels, per_device(): pl.pallas_call(collide_kernel, name='collide', out_shape=(shape(3, SLOTS,...  2.34 us

profile of v9, /device:TPU:1, one launch (start us, length us, event | category | flops | bytes accessed | tf_op | source)
XLA Modules:
  0.0 17.7 jit_solution(10442619961698442786)
XLA Ops:
  0.6 14.7 %prep.1 = (f32[264,128]{1,0:T(8,128)S(1)}, f32[2,56,128]{2,1,0:T(8,128)S(1)}, f32[64,128]{1,0:T(8,128)S(1)}, f32[3,24,256]{2,1,0:T(8,128)S(1)}, f32[4,64,128]{2,...) custom-call(s32[4]{0:T(128)} %bitcast.9, s32[3]{0:T(128)} %shift_in.3, ...), custom_call_target="tpu_custom_call" | custom-call | tf_op jit(solution)/shard_map/prep/pallas_call | solution.py:486
  15.3 2.3 %collide.1 = (f32[3,96,128]{2,1,0:T(8,128)}, f32[3,64,128]{2,1,0:T(8,128)}) custom-call(s32[3]{0:T(128)} %shift_in.3, f32[264,128]{1,0:T(8,128)S(1)} %get-tuple-element.12.border, f32[2,56,128]{2,1,0:T(8,128)S(1)} %get-tuple-element.13.own_axis, f32[64,128]{1,0:T(8,128)S(1)} %get-tuple-element.14.ids, f32[3,24,256]{2,1,0:T(8,128)S(1)} %get-tuple-element.15.inner_mean, ...), custom_call_target="tpu_custom_call" | custom-call | tf_op jit(solution)/shard_map/collide/pallas_call | solution.py:522

commit v10 on v5

--- a/solution.py
+++ b/solution.py
@@ -336,7 +336,7 @@
 ):
     load = pltpu.make_async_copy(shift_in, shift, load_sem)
     load.start()
-    total[...] = border[...]
+    total[0 : 8 * BORDER, :] = border[0 : 8 * BORDER, :]
     for k, places in enumerate(
         (
             ((24, 0, 2), (18, 2, 6), (16, 8, 2)),
@@ -383,11 +383,12 @@
         number = looked[3].astype(jnp.int32)
         bits = [(number & (1 << k)) != 0 for k in range(4)]
         a = []
-        for c in range(3):
+        for c in range(2):
             level = [entry[c] for entry in choices]
             for k in range(4):
                 level = [jnp.where(bits[k], level[2 * m + 1], level[2 * m]) for m in range(len(level) // 2)]
             a.append(level[0])
+        a.append((1.0 - 1.0 / NAX) - (2.0 / NAX) * looked[3])
         w = [v[c] - mean[c] for c in range(3)]
         cross = [
             a[1] * w[2] - a[2] * w[1],
@@ -483,7 +484,7 @@
         prep_kernel,
         name="prep",
         out_shape=(
-            shape(8 * BORDER, 128),
+            shape(8 * BORDER + 8, 128),
             shape(2, 56, 128),
             shape(ROWS, 128),
             shape(3, 24, 256),
@@ -502,9 +503,9 @@
             pltpu.VMEM((ROWS, 128), F32),
             pltpu.VMEM((ROWS, 128), F32),
             pltpu.VMEM((7 * MAIN + 16, 256), F32),
-            pltpu.VMEM((2, 128, 128), F32),
+            pltpu.VMEM((2, 136, 128), F32),
             pltpu.VMEM((32, 128), F32),
-            pltpu.VMEM((128, 128), F32),
+            pltpu.VMEM((144, 128), F32),
             pltpu.VMEM((4, 144, 128), F32),
             pltpu.VMEM((4, 24, 128), F32),
             pltpu.SemaphoreType.DMA((5,)),
@@ -525,8 +526,8 @@
             pltpu.SMEM((3,), jnp.int32),
             pltpu.VMEM((3, SLOTS, 128), F32),
             pltpu.VMEM((3, 64, 128), F32),
-            pltpu.VMEM((8 * BORDER, 128), F32),
-            pltpu.VMEM((3, 104, 128), F32),
+            pltpu.VMEM((8 * BORDER + 8, 128), F32),
+            pltpu.VMEM((3, 112, 128), F32),
             pltpu.SemaphoreType.DMA,
             pltpu.SemaphoreType.DMA((3,)),
         ],

time: 17.8 us -> 17.8 us (level)
  no operation moved by 1% of the time
where the time goes in v10:
time: 17.8 us; the launch traced here: 17.6 us
  Pallas kernels  17 us (96%)
  between operations  0.64 us (4%)
    pallas_call x1, Pallas kernels, per_device(): pl.pallas_call(prep_kernel, name='prep', out_shape=(shape(8 * BORDER + 8,...  14.7 us
    pallas_call x1, Pallas kernels, per_device(): pl.pallas_call(collide_kernel, name='collide', out_shape=(shape(3, SLOTS,...  2.31 us

profile of v10, /device:TPU:1, one launch (start us, length us, event | category | flops | bytes accessed | tf_op | source)
XLA Modules:
  0.0 17.6 jit_solution(17359134732477980202)
XLA Ops:
  0.6 14.7 %prep.1 = (f32[264,128]{1,0:T(8,128)S(1)}, f32[2,56,128]{2,1,0:T(8,128)S(1)}, f32[64,128]{1,0:T(8,128)S(1)}, f32[3,24,256]{2,1,0:T(8,128)S(1)}, f32[4,64,128]{2,...) custom-call(s32[4]{0:T(128)} %bitcast.9, s32[3]{0:T(128)} %shift_in.3, ...), custom_call_target="tpu_custom_call" | custom-call | tf_op jit(solution)/shard_map/prep/pallas_call | solution.py:483
  15.3 2.3 %collide.1 = (f32[3,96,128]{2,1,0:T(8,128)}, f32[3,64,128]{2,1,0:T(8,128)}) custom-call(s32[3]{0:T(128)} %shift_in.3, f32[264,128]{1,0:T(8,128)S(1)} %get-tuple-element.12.border, f32[2,56,128]{2,1,0:T(8,128)S(1)} %get-tuple-element.13.own_axis, f32[64,128]{1,0:T(8,128)S(1)} %get-tuple-element.14.ids, f32[3,24,256]{2,1,0:T(8,128)S(1)} %get-tuple-element.15.inner_mean, ...), custom_call_target="tpu_custom_call" | custom-call | tf_op jit(solution)/shard_map/collide/pallas_call | solution.py:519

commit v11 on v10

--- a/solution.py
+++ b/solution.py
@@ -124,7 +124,9 @@
     for target in targets:
         pl.semaphore_signal(barrier, inc=1, device_id=target, device_id_type=MESH)
     axis_s[...] = jnp.zeros(axis_s.shape, F32)
-    side[:, 112:144, :] = jnp.zeros((4, 32, 128), F32)
+    for k in (0, 2):
+        side[k, 112:144, :] = jnp.zeros((32, 128), F32)
+    corner[:, 20:24, :] = jnp.zeros((4, 4, 128), F32)
     for load in loads:
         load.wait()
 
@@ -206,15 +208,12 @@
             own_axis[par, first : first + n, :] = axis_s[pl.ds(start, n, stride=step), :]
         own_axis[par, 50:56, :] = jnp.zeros((6, 128), F32)
         base = 112 + 16 * par
-        for k, order in enumerate(
-            (((8, 2), (2, 6), (0, 2)), ((24, 2), (18, 6), (16, 2)), ((0, 2), (26, 6), (24, 2)), ((16, 2), (10, 6), (8, 2)))
-        ):
+        for k, order in ((0, ((8, 2), (2, 6), (0, 2))), (2, ((0, 2), (26, 6), (24, 2)))):
             at = base
             for first, n in order:
                 side[k, at : at + n, :] = own_axis[par, first : first + n, :]
                 at += n
-        for k, first in enumerate((0, 8, 24, 16)):
-            corner[k, 20 + 2 * par : 22 + 2 * par, :] = own_axis[par, first : first + 2, :]
+        corner[0, 20 + 2 * par : 22 + 2 * par, :] = own_axis[par, 0:2, :]
 
     slot = iota((8, 128), 0) * 128 + iota((8, 128), 1)
     lane = iota((8, 128), 1)
@@ -290,7 +289,11 @@
     pl.semaphore_wait(barrier, 8)
     copies = []
     for k in (4, 5, 6, 7, 0, 1, 2, 3):
-        source, target = (side.at[k], got_side.at[k]) if k < 4 else (corner.at[k - 4], got_corner.at[k - 4])
+        if k < 4:
+            size = 144 if k in (0, 2) else 112
+            source, target = side.at[k, pl.ds(0, size), :], got_side.at[k, pl.ds(0, size), :]
+        else:
+            source, target = corner.at[k - 4], got_corner.at[k - 4]
         copy = pltpu.make_async_remote_copy(
             src_ref=source,
             dst_ref=target,
@@ -353,17 +356,11 @@
     for par in range(2):
         number = own_axis[par, 0:BORDER, :]
         at = 112 + 16 * par
-        zero = jnp.zeros((16, 128), F32)
-        for k, (before, after) in enumerate(((16, 0), (0, 16), (8, 8))):
-            strip = got_side[k, at : at + 16, :]
-            parts = [jnp.zeros((before, 128), F32)] * (before > 0) + [strip]
-            parts += [jnp.zeros((after, 128), F32)] * (after > 0)
-            number = number + jnp.concatenate(parts, 0)
-        strip = got_side[3, at : at + 16, :]
-        number = number + jnp.concatenate([strip[8:16], zero, strip[0:8]], 0)
-        pair = [got_corner[k, 20 + 2 * par : 22 + 2 * par, :] for k in range(4)]
-        gap = jnp.zeros((6, 128), F32)
-        number = number + jnp.concatenate([pair[3], gap, pair[2], gap, pair[0], gap, pair[1], gap], 0)
+        gap = jnp.zeros((16, 128), F32)
+        number = number + jnp.concatenate([gap, got_side[0, at : at + 16, :]], 0)
+        number = number + jnp.concatenate([gap[0:8], got_side[2, at : at + 16, :], gap[0:8]], 0)
+        pair = got_corner[0, 20 + 2 * par : 22 + 2 * par, :]
+        number = number + jnp.concatenate([gap, pair, gap[0:14]], 0)
         numbers.append(number)
     groups = [None] * 7
     most = [jnp.maximum(total[pl.ds(par, BORDER, stride=8), :], 1.0) for par in range(2)]

time: 17.8 us -> 17.8 us (level)
  no operation moved by 1% of the time
where the time goes in v11:
time: 17.8 us; the launch traced here: 17.7 us
  Pallas kernels  17 us (96%)
  between operations  0.64 us (4%)
    pallas_call x1, Pallas kernels, per_device(): pl.pallas_call(prep_kernel, name='prep', out_shape=(shape(8 * BORDER + 8,...  14.7 us
    pallas_call x1, Pallas kernels, per_device(): pl.pallas_call(collide_kernel, name='collide', out_shape=(shape(3, SLOTS,...  2.32 us

profile of v11, /device:TPU:1, one launch (start us, length us, event | category | flops | bytes accessed | tf_op | source)
XLA Modules:
  0.0 17.7 jit_solution(8573279458012274771)
XLA Ops:
  0.6 14.7 %prep.1 = (f32[264,128]{1,0:T(8,128)S(1)}, f32[2,56,128]{2,1,0:T(8,128)S(1)}, f32[64,128]{1,0:T(8,128)S(1)}, f32[3,24,256]{2,1,0:T(8,128)S(1)}, f32[4,64,128]{2,...) custom-call(s32[4]{0:T(128)} %bitcast.9, s32[3]{0:T(128)} %shift_in.3, ...), custom_call_target="tpu_custom_call" | custom-call | tf_op jit(solution)/shard_map/prep/pallas_call | solution.py:480
  15.3 2.3 %collide.1 = (f32[3,96,128]{2,1,0:T(8,128)}, f32[3,64,128]{2,1,0:T(8,128)}) custom-call(s32[3]{0:T(128)} %shift_in.3, f32[264,128]{1,0:T(8,128)S(1)} %get-tuple-element.12.border, f32[2,56,128]{2,1,0:T(8,128)S(1)} %get-tuple-element.13.own_axis, f32[64,128]{1,0:T(8,128)S(1)} %get-tuple-element.14.ids, f32[3,24,256]{2,1,0:T(8,128)S(1)} %get-tuple-element.15.inner_mean, ...), custom_call_target="tpu_custom_call" | custom-call | tf_op jit(solution)/shard_map/collide/pallas_call | solution.py:516

commit v12 on v10

--- a/solution.py
+++ b/solution.py
@@ -107,7 +107,7 @@
 
 def prep_kernel(
     leaving_in, shift_in, vel_in, pos_in, axis_in,
-    border, own_axis, ids, inner_mean, found, vel, got_side, got_corner,
+    border, own_axis, ids, inner_means, found, vel, got_side, got_corner,
     leaving, shift, pos, axis, row_s, col_s, sums, run_s, prep_s, axis_s, side, corner,
     load_sem, send_sem, recv_sem,
 ):
@@ -311,7 +311,12 @@
     high_rows, low_rows = [], []
     for c in range(3):
         mean = (inner(1 + 2 * c) + inner(2 + 2 * c)) / most
-        inner_mean[c] = mean
+        inner_means[c] = jnp.zeros((112, 128), F32)
+        for par in range(2):
+            for w in range(6):
+                start = (2 + w) * 10 + 2 + par
+                piece = mean[3 * w : 3 * w + 3, 128 * par : 128 * par + 128]
+                inner_means[c, pl.ds(start, 3, stride=2), :] = piece
         high = high_part(mean)
         high_rows.append(high)
         low_rows.append(mean - high)
@@ -330,7 +335,7 @@
 
 
 def collide_kernel(
-    shift_in, border, own_axis, ids, inner_mean, found, vel, got_side, got_corner,
+    shift_in, border, own_axis, ids, inner_means, found, vel, got_side, got_corner,
     out_hbm, flow_hbm,
     shift, out, flow, total, means, load_sem, store_sem,
 ):
@@ -445,14 +450,14 @@
         turn(slice(at, at + 8), v[3] >= 0.0, v, looked)
     store(out, out_hbm)
 
+    means[...] = inner_means[...]
     for c in range(3):
         for par in range(2):
             lanes = slice(par * 128, par * 128 + 128)
             for first, n, cx, cx_step, half_y, half_step in PIECES:
-                if first < BORDER:
-                    piece = border_mean[c][first : first + n, lanes]
-                else:
-                    piece = inner_mean[c, first - BORDER : first - BORDER + n, lanes]
+                if first >= BORDER:
+                    continue
+                piece = border_mean[c][first : first + n, lanes]
                 start = cx * 10 + 2 * half_y + par
                 means[c, pl.ds(start, n, stride=10 * cx_step + 2 * half_step), :] = piece
     load.wait()
@@ -487,7 +492,7 @@
             shape(8 * BORDER + 8, 128),
             shape(2, 56, 128),
             shape(ROWS, 128),
-            shape(3, 24, 256),
+            shape(3, 112, 128),
             shape(4, ROWS, 128),
             shape(3, ROWS, 128),
             shape(4, 144, 128),

time: 17.8 us -> 17.8 us (level)
  no operation moved by 1% of the time
where the time goes in v12:
time: 17.8 us; the launch traced here: 17.6 us
  Pallas kernels  17 us (96%)
  between operations  0.64 us (4%)
    pallas_call x1, Pallas kernels, per_device(): pl.pallas_call(prep_kernel, name='prep', out_shape=(shape(8 * BORDER + 8,...  14.7 us
    pallas_call x1, Pallas kernels, per_device(): pl.pallas_call(collide_kernel, name='collide', out_shape=(shape(3, SLOTS,...  2.31 us

profile of v12, /device:TPU:1, one launch (start us, length us, event | category | flops | bytes accessed | tf_op | source)
XLA Modules:
  0.0 17.6 jit_solution(2468439423584406470)
XLA Ops:
  0.6 14.7 %prep.1 = (f32[264,128]{1,0:T(8,128)S(1)}, f32[2,56,128]{2,1,0:T(8,128)S(1)}, f32[64,128]{1,0:T(8,128)S(1)}, f32[3,112,128]{2,1,0:T(8,128)S(1)}, f32[4,64,128]{2...) custom-call(s32[4]{0:T(128)} %bitcast.9, s32[3]{0:T(128)} %shift_in.3, ...), custom_call_target="tpu_custom_call" | custom-call | tf_op jit(solution)/shard_map/prep/pallas_call | solution.py:488
  15.3 2.3 %collide.1 = (f32[3,96,128]{2,1,0:T(8,128)}, f32[3,64,128]{2,1,0:T(8,128)}) custom-call(s32[3]{0:T(128)} %shift_in.3, f32[264,128]{1,0:T(8,128)S(1)} %get-tuple-element.12.border, f32[2,56,128]{2,1,0:T(8,128)S(1)} %get-tuple-element.13.own_axis, f32[64,128]{1,0:T(8,128)S(1)} %get-tuple-element.14.ids, f32[3,112,128]{2,1,0:T(8,128)S(1)} %get-tuple-element.15.inner_means, ...), custom_call_target="tpu_custom_call" | custom-call | tf_op jit(solution)/shard_map/collide/pallas_call | solution.py:524

commit v13 on v12

--- a/solution.py
+++ b/solution.py
@@ -331,7 +331,9 @@
     place = iota((ROWS, 128), 0) * 128 + iota((ROWS, 128), 1)
     ids[...] = jnp.where(place >= gone, ids[...], -1.0)
     for copy in copies:
-        copy.wait()
+        copy.wait_send()
+    for copy in copies[4:] + copies[:4]:
+        copy.wait_recv()
 
 
 def collide_kernel(

time: 17.8 us -> 17.7 us (level)
  no operation moved by 1% of the time
where the time goes in v13:
time: 17.7 us; the launch traced here: 17.6 us
  Pallas kernels  17 us (96%)
  between operations  0.64 us (4%)
    pallas_call x1, Pallas kernels, per_device(): pl.pallas_call(prep_kernel, name='prep', out_shape=(shape(8 * BORDER + 8,...  14.7 us
    pallas_call x1, Pallas kernels, per_device(): pl.pallas_call(collide_kernel, name='collide', out_shape=(shape(3, SLOTS,...  2.31 us

profile of v13, /device:TPU:1, one launch (start us, length us, event | category | flops | bytes accessed | tf_op | source)
XLA Modules:
  0.0 17.6 jit_solution(4395082366055130597)
XLA Ops:
  0.6 14.7 %prep.1 = (f32[264,128]{1,0:T(8,128)S(1)}, f32[2,56,128]{2,1,0:T(8,128)S(1)}, f32[64,128]{1,0:T(8,128)S(1)}, f32[3,112,128]{2,1,0:T(8,128)S(1)}, f32[4,64,128]{2...) custom-call(s32[4]{0:T(128)} %bitcast.9, s32[3]{0:T(128)} %shift_in.3, ...), custom_call_target="tpu_custom_call" | custom-call | tf_op jit(solution)/shard_map/prep/pallas_call | solution.py:490
  15.3 2.3 %collide.1 = (f32[3,96,128]{2,1,0:T(8,128)}, f32[3,64,128]{2,1,0:T(8,128)}) custom-call(s32[3]{0:T(128)} %shift_in.3, f32[264,128]{1,0:T(8,128)S(1)} %get-tuple-element.12.border, f32[2,56,128]{2,1,0:T(8,128)S(1)} %get-tuple-element.13.own_axis, f32[64,128]{1,0:T(8,128)S(1)} %get-tuple-element.14.ids, f32[3,112,128]{2,1,0:T(8,128)S(1)} %get-tuple-element.15.inner_means, ...), custom_call_target="tpu_custom_call" | custom-call | tf_op jit(solution)/shard_map/collide/pallas_call | solution.py:526

commit v14 on v11

--- a/solution.py
+++ b/solution.py
@@ -107,7 +107,7 @@
 
 def prep_kernel(
     leaving_in, shift_in, vel_in, pos_in, axis_in,
-    border, own_axis, ids, inner_mean, found, vel, got_side, got_corner,
+    border, own_axis, ids, inner_means, found, vel, got_side, got_corner,
     leaving, shift, pos, axis, row_s, col_s, sums, run_s, prep_s, axis_s, side, corner,
     load_sem, send_sem, recv_sem,
 ):
@@ -314,7 +314,12 @@
     high_rows, low_rows = [], []
     for c in range(3):
         mean = (inner(1 + 2 * c) + inner(2 + 2 * c)) / most
-        inner_mean[c] = mean
+        inner_means[c] = jnp.zeros((112, 128), F32)
+        for par in range(2):
+            for w in range(6):
+                start = (2 + w) * 10 + 2 + par
+                piece = mean[3 * w : 3 * w + 3, 128 * par : 128 * par + 128]
+                inner_means[c, pl.ds(start, 3, stride=2), :] = piece
         high = high_part(mean)
         high_rows.append(high)
         low_rows.append(mean - high)
@@ -333,7 +338,7 @@
 
 
 def collide_kernel(
-    shift_in, border, own_axis, ids, inner_mean, found, vel, got_side, got_corner,
+    shift_in, border, own_axis, ids, inner_means, found, vel, got_side, got_corner,
     out_hbm, flow_hbm,
     shift, out, flow, total, means, load_sem, store_sem,
 ):
@@ -442,14 +447,14 @@
         turn(slice(at, at + 8), v[3] >= 0.0, v, looked)
     store(out, out_hbm)
 
+    means[...] = inner_means[...]
     for c in range(3):
         for par in range(2):
             lanes = slice(par * 128, par * 128 + 128)
             for first, n, cx, cx_step, half_y, half_step in PIECES:
-                if first < BORDER:
-                    piece = border_mean[c][first : first + n, lanes]
-                else:
-                    piece = inner_mean[c, first - BORDER : first - BORDER + n, lanes]
+                if first >= BORDER:
+                    continue
+                piece = border_mean[c][first : first + n, lanes]
                 start = cx * 10 + 2 * half_y + par
                 means[c, pl.ds(start, n, stride=10 * cx_step + 2 * half_step), :] = piece
     load.wait()
@@ -484,7 +489,7 @@
             shape(8 * BORDER + 8, 128),
             shape(2, 56, 128),
             shape(ROWS, 128),
-            shape(3, 24, 256),
+            shape(3, 112, 128),
             shape(4, ROWS, 128),
             shape(3, ROWS, 128),
             shape(4, 144, 128),

time: 17.8 us -> 17.8 us (level)
  no operation moved by 1% of the time
where the time goes in v14:
time: 17.8 us; the launch traced here: 17.7 us
  Pallas kernels  17 us (96%)
  between operations  0.64 us (4%)
    pallas_call x1, Pallas kernels, per_device(): pl.pallas_call(prep_kernel, name='prep', out_shape=(shape(8 * BORDER + 8,...  14.7 us
    pallas_call x1, Pallas kernels, per_device(): pl.pallas_call(collide_kernel, name='collide', out_shape=(shape(3, SLOTS,...  2.32 us

profile of v14, /device:TPU:1, one launch (start us, length us, event | category | flops | bytes accessed | tf_op | source)
XLA Modules:
  0.0 17.7 jit_solution(4165549158969640753)
XLA Ops:
  0.6 14.7 %prep.1 = (f32[264,128]{1,0:T(8,128)S(1)}, f32[2,56,128]{2,1,0:T(8,128)S(1)}, f32[64,128]{1,0:T(8,128)S(1)}, f32[3,112,128]{2,1,0:T(8,128)S(1)}, f32[4,64,128]{2...) custom-call(s32[4]{0:T(128)} %bitcast.9, s32[3]{0:T(128)} %shift_in.3, ...), custom_call_target="tpu_custom_call" | custom-call | tf_op jit(solution)/shard_map/prep/pallas_call | solution.py:485
  15.3 2.3 %collide.1 = (f32[3,96,128]{2,1,0:T(8,128)}, f32[3,64,128]{2,1,0:T(8,128)}) custom-call(s32[3]{0:T(128)} %shift_in.3, f32[264,128]{1,0:T(8,128)S(1)} %get-tuple-element.12.border, f32[2,56,128]{2,1,0:T(8,128)S(1)} %get-tuple-element.13.own_axis, f32[64,128]{1,0:T(8,128)S(1)} %get-tuple-element.14.ids, f32[3,112,128]{2,1,0:T(8,128)S(1)} %get-tuple-element.15.inner_means, ...), custom_call_target="tpu_custom_call" | custom-call | tf_op jit(solution)/shard_map/collide/pallas_call | solution.py:521
